TPU v7x, 512 devices: a whole 4x4x16 slice. The times are simulated.
512 devices in a mesh: req: 128 (over x, z, core), ctx: 4 (over y).
Axes of the slice: x: 4, y: 4, z: 16, core: 2. Of those that a mesh axis runs over, the one named last changes fastest.
Arguments:
- prefill_residual: bfloat16 [131072, 1536], P(('req', 'ctx')), may hold values from -1.75 to 1.75
- prompt_queries: bfloat16 [131072, 1536], P(('req', 'ctx')), may hold values from -100 to 100
- prompt_keys: bfloat16 [131072, 512], P(('req', 'ctx')), may hold values from -12 to 12
- prompt_values: bfloat16 [131072, 512], P(('req', 'ctx')), may hold values from -6 to 6
- out_weight: bfloat16 [1536, 1536], P(None, 'ctx'), may hold values from -0.15625 to 0.15625
- prompt_token_counts: int32 [128, 3], P('req'), may hold values from 1 to 512, 1024 in all within a row
- page_dest: int32 [128, 128, 1], P('req'), may hold values from 0 to 127; in each aligned block of 128 rows (0 to 127, 128 to 255, ..., all dimensions but the last counted through in order) at most 2 rows name the same one
- decode_residual: bfloat16 [128, 3, 1536], P('req', None, 'ctx'), may hold values from -1.75 to 1.75
- decoded_queries: bfloat16 [128, 3, 1536], P('req', None, 'ctx'), may hold values from -300 to 300
- decoded_keys: bfloat16 [128, 3, 512], P('req', None, 'ctx'), may hold values from -12 to 12
- decoded_values: bfloat16 [128, 3, 512], P('req', None, 'ctx'), may hold values from -6 to 6
Outputs:
- prefill_out: bfloat16 [131072, 1536], P(('req', 'ctx'))
- target_page_store: bfloat16 [128, 256, 8, 2, 512], P('req', None, None, None, 'ctx')
- decode_out: bfloat16 [128, 3, 1536], P('req', None, 'ctx')
Inputs may be any that keep to these rules, and one draw needn't show every extreme that they name: `prompt_token_counts`: each row sums to 1024; the largest prompt of every group has exactly 512 tokens. `page_dest`: at most 2 pages of one group go to one destination group, and in every draw some group sends exactly 2 pages to one destination.
All inputs are finite; a program needn't handle non-finite values.
Results may differ from a plain program's by a relative error of at most 0.0075.
Values may be sent and summed in bfloat16 or wider, within the bound.
No kernel may reach another device: no remote copies, remote signals or barrier semaphores. Data moves between devices by JAX's collectives and lax.ppermute only.
A program may use at most 128 MiB of HBM per device.

v0:
```python
import math

import jax
import jax.numpy as jnp
from jax import lax
from jax.sharding import PartitionSpec as P

QUERY_HEADS = 24
KEY_VALUE_HEADS = 8
HEAD_SIZE = 64
PAGE_TOKENS = 8


masked_score = -1e30


def prompt_ids(lengths_row, positions):
    prompt_ends = jnp.cumsum(lengths_row)
    return jnp.sum((positions[:, None] >= prompt_ends[None, :]).astype(jnp.int32), axis=1)


def blank_state(query_rows, kv_count, queries_per_key_head):
    return (
        jnp.full((query_rows, kv_count, queries_per_key_head), masked_score, jnp.float32),
        jnp.zeros((query_rows, kv_count, queries_per_key_head), jnp.float32),
        jnp.zeros((query_rows, kv_count, queries_per_key_head, HEAD_SIZE), jnp.float32),
    )


def sweep_keys(carry_state, query_grouped, q_pos, q_prompt, k_all, v_all, lengths_row, logit_scale):
    key_count = k_all.shape[0]
    block_rows = math.gcd(key_count, 512)
    block_count = key_count // block_rows
    k_blocks = k_all.reshape(block_count, block_rows, k_all.shape[1], HEAD_SIZE)
    v_blocks = v_all.reshape(block_count, block_rows, v_all.shape[1], HEAD_SIZE)

    def advance(state_now, inputs):
        k_block, v_block, block_index = inputs
        row_max, total, weighted = state_now
        k_pos = block_index * block_rows + jnp.arange(block_rows, dtype=jnp.int32)
        k_prompt = prompt_ids(lengths_row, k_pos)
        allowed = (q_prompt[:, None] == k_prompt[None, :]) & (k_pos[None, :] <= q_pos[:, None])
        visible = allowed[:, None, None, :]
        scores = (
            jnp.einsum("tgrd,bgd->tgrb", query_grouped, k_block, preferred_element_type=jnp.float32)
            * logit_scale
        )
        scores = jnp.where(visible, scores, masked_score)
        new_max = jnp.maximum(row_max, jnp.max(scores, axis=-1))
        factor = jnp.exp(row_max - new_max)
        weights = jnp.where(visible, jnp.exp(scores - new_max[..., None]), 0.0)
        total = total * factor + jnp.sum(weights, axis=-1)
        weighted = weighted * factor[..., None] + jnp.einsum(
            "tgrb,bgd->tgrd",
            weights.astype(jnp.bfloat16),
            v_block,
            preferred_element_type=jnp.float32,
        )
        return ((new_max, total, weighted), None)

    final_state, unused = lax.scan(
        advance, carry_state, (k_blocks, v_blocks, jnp.arange(block_count, dtype=jnp.int32))
    )
    return final_state


def shards(
    prefill_residual,
    prompt_queries,
    prompt_keys,
    prompt_values,
    out_weight,
    prompt_token_counts,
    page_dest,
    decode_residual,
    decoded_queries,
    decoded_keys,
    decoded_values,
):
    context_count = lax.axis_size("ctx")
    n_req = lax.axis_size("req")
    token_rows = prefill_residual.shape[0]
    group_rows = token_rows * context_count
    queries_per_key_head = QUERY_HEADS // KEY_VALUE_HEADS
    resident_key_value = KEY_VALUE_HEADS // context_count
    local_q = QUERY_HEADS // context_count
    logit_scale = 1.0 / math.sqrt(HEAD_SIZE)
    lengths_row = prompt_token_counts[0]
    kv_cols = prompt_keys.shape[1] // context_count
    ctx_index = lax.axis_index("ctx")
    packed = jnp.stack([prompt_keys, prompt_values], axis=1).reshape(
        token_rows, 2, context_count, kv_cols
    )
    q_pos = ctx_index * token_rows + jnp.arange(token_rows, dtype=jnp.int32)
    q_prompt = prompt_ids(lengths_row, q_pos)
    query_grouped = prompt_queries.reshape(
        token_rows, KEY_VALUE_HEADS, queries_per_key_head, HEAD_SIZE
    )
    key_portion = lax.all_gather(prompt_keys, "ctx", axis=0, tiled=True)
    value_portion = lax.all_gather(prompt_values, "ctx", axis=0, tiled=True)
    row_max, total, weighted = sweep_keys(
        blank_state(token_rows, KEY_VALUE_HEADS, queries_per_key_head),
        query_grouped,
        q_pos,
        q_prompt,
        key_portion.reshape(-1, KEY_VALUE_HEADS, HEAD_SIZE),
        value_portion.reshape(-1, KEY_VALUE_HEADS, HEAD_SIZE),
        lengths_row,
        logit_scale,
    )
    attention = (
        (weighted / total[..., None])
        .reshape(token_rows, QUERY_HEADS * HEAD_SIZE)
        .astype(jnp.bfloat16)
    )
    kv_local = lax.all_to_all(packed, "ctx", split_axis=2, concat_axis=0, tiled=True).reshape(
        group_rows, 2, kv_cols
    )
    key_group = kv_local[:, 0].reshape(group_rows, resident_key_value, HEAD_SIZE)
    value_group = kv_local[:, 1].reshape(group_rows, resident_key_value, HEAD_SIZE)
    request_count = decoded_queries.shape[1]
    all_prompt = prompt_ids(lengths_row, jnp.arange(group_rows, dtype=jnp.int32))
    fresh_query_grouped = decoded_queries[0].reshape(
        request_count, resident_key_value, queries_per_key_head, HEAD_SIZE
    )
    dec_scores = (
        jnp.einsum(
            "rgqd,mgd->rgqm", fresh_query_grouped, key_group, preferred_element_type=jnp.float32
        )
        * logit_scale
    )
    dec_visible = (all_prompt[None, :] == jnp.arange(request_count, dtype=jnp.int32)[:, None])[
        :, None, None, :
    ]
    dec_scores = jnp.where(dec_visible, dec_scores, masked_score)
    self_score = (
        jnp.sum(
            fresh_query_grouped.astype(jnp.float32)
            * decoded_keys[0]
            .reshape(request_count, resident_key_value, 1, HEAD_SIZE)
            .astype(jnp.float32),
            axis=-1,
        )
        * logit_scale
    )
    dec_max = jnp.maximum(jnp.max(dec_scores, axis=-1), self_score)
    dec_weights = jnp.where(dec_visible, jnp.exp(dec_scores - dec_max[..., None]), 0.0)
    self_weight = jnp.exp(self_score - dec_max)
    dec_total = jnp.sum(dec_weights, axis=-1) + self_weight
    decode_weighted_sum = jnp.einsum(
        "rgqm,mgd->rgqd",
        dec_weights.astype(jnp.bfloat16),
        value_group,
        preferred_element_type=jnp.float32,
    )
    decode_weighted_sum = decode_weighted_sum + self_weight.astype(jnp.bfloat16).astype(
        jnp.float32
    )[..., None] * decoded_values[0].reshape(
        request_count, resident_key_value, 1, HEAD_SIZE
    ).astype(
        jnp.float32
    )
    new_attention = (
        (decode_weighted_sum / dec_total[..., None])
        .reshape(request_count, local_q * HEAD_SIZE)
        .astype(jnp.bfloat16)
    )
    padded_new = jnp.zeros((request_count, prompt_queries.shape[1]), jnp.bfloat16)
    padded_new = lax.dynamic_update_slice_in_dim(
        padded_new, new_attention, ctx_index * local_q * HEAD_SIZE, 1
    )
    left_side = jnp.concatenate([attention, padded_new], axis=0)
    products = jnp.dot(
        left_side,
        lax.all_gather(out_weight, "ctx", axis=1, tiled=True),
        preferred_element_type=jnp.float32,
    )
    prefill_out = (prefill_residual.astype(jnp.float32) + products[:token_rows]).astype(
        jnp.bfloat16
    )
    summed = lax.psum_scatter(products[token_rows:], "ctx", scatter_dimension=1, tiled=True)
    decode_out = (decode_residual[0].astype(jnp.float32) + summed).astype(jnp.bfloat16)[None]
    page_count = group_rows // PAGE_TOKENS
    lane_cap = max(2, 2 * page_count // n_req)
    key_value_pages = kv_local.reshape(page_count, PAGE_TOKENS, 2, kv_cols)
    target_group = page_dest[0, :, 0]
    marks = (target_group[:, None] == jnp.arange(n_req, dtype=jnp.int32)[None, :]).astype(jnp.int32)
    earlier = jnp.cumsum(marks, axis=0) - marks
    in_lane = jnp.sum(earlier * marks, axis=1)
    outgoing = (
        jnp.zeros((n_req * lane_cap, PAGE_TOKENS, 2, kv_cols), jnp.bfloat16)
        .at[target_group * lane_cap + in_lane]
        .set(key_value_pages)
    )
    target_page_store = lax.all_to_all(outgoing, "req", split_axis=0, concat_axis=0, tiled=True)[
        None
    ]
    return (prefill_out, target_page_store, decode_out)


def solution(mesh):
    in_specs = (
        P(("req", "ctx"), None),
        P(("req", "ctx"), None),
        P(("req", "ctx"), None),
        P(("req", "ctx"), None),
        P(None, "ctx"),
        P("req", None),
        P("req", None, None),
        P("req", None, "ctx"),
        P("req", None, "ctx"),
        P("req", None, "ctx"),
        P("req", None, "ctx"),
    )
    out_specs = (P(("req", "ctx"), None), P("req", None, None, None, "ctx"), P("req", None, "ctx"))
    return jax.shard_map(shards, mesh=mesh, in_specs=in_specs, out_specs=out_specs, check_vma=False)
```

profile of v0, /device:TPU:4, one launch (start us, length us, event | category | flops | bytes accessed | tf_op | source)
XLA Modules:
  0.0 187.7 jit_solution(7827996466309464005)
XLA Ops:
  11.8 4.5 %all-to-all-start = ((bf16[256,2,4,128]{0,3,1,2:T(8,128)(2,1)}), bf16[256,2,4,128]{0,3,1,2:T(8,128)(2,1)S(1)}, u32[]{:S(2)}, u32[]{:S(2)}) async-start(bf16[256,2,4,128]{0,3,1,2:T(8,128)(2,1)} %copy.115), calls=%async_computation | async-start | bytes 1048576 | tf_op jit(solution)/shard_map/all_to_all | solution.py:116
  18.7 7.1 %all-to-all-done = bf16[256,2,4,128]{0,3,1,2:T(8,128)(2,1)S(1)} async-done(((bf16[256,2,4,128]{0,3,1,2:T(8,128)(2,1)}), bf16[256,2,4,128]{0,3,1,2:T(8,128)(2,1)S(1)}, u32[]{:S(2)}, u32[]{:S(2)}) %all-to-all-start) | async-done | bytes 524320 | tf_op jit(solution)/shard_map/all_to_all | solution.py:116
  28.5 12.3 %scatter_fusion = bf16[256,8,2,128]{3,1,2,0:T(8,128)(2,1)} fusion(bf16[256,8,2,128]{3,1,2,0:T(8,128)(2,1)} %broadcast_in_dim.98, s32[128]{0:T(128)S(1)} %fusion.43, bf16[128,8,2,128]{3,1,2,0:T(8,128)(2,1)S(1)} %copy.124), kind=kCustom, calls=%fused_computation | custom fusion | bytes 1573376 | tf_op jit(solution)/shard_map/scatter | solution.py:193
  40.8 19.8 %all-to-all-start.1 = ((bf16[256,8,2,128]{3,1,2,0:T(8,128)(2,1)}), bf16[256,8,2,128]{3,1,2,0:T(8,128)(2,1)S(1)}, u32[]{:S(2)}, u32[]{:S(2)}) async-start(bf16[256,8,2,128]{3,1,2,0:T(8,128)(2,1)} %scatter_fusion), calls=%async_computation.1 | async-start | bytes 2097152 | tf_op jit(solution)/shard_map/all_to_all | solution.py:195
  60.9 3.9 %reshape.230 = bf16[2,512,8,64]{3,2,1,0:T(8,128)(2,1)} reshape(bf16[1024,512]{1,0:T(8,128)(2,1)} %all-gather.4.cloned.1.call-done) | data formatting | bytes 2097152 | tf_op jit(solution)/shard_map/reshape;reshape | solution.py:34
  64.9 2.5 %copy.111 = bf16[2,512,8,64]{1,3,2,0:T(8,128)(2,1)S(1)} copy(bf16[2,512,8,64]{3,2,1,0:T(8,128)(2,1)} %reshape.230) | data formatting | bytes 2097152
  67.4 13.1 %all-gather.6.cloned.1.call-done = bf16[1024,512]{1,0:T(8,128)(2,1)} async-done(((bf16[256,512]{1,0:T(8,128)(2,1)}), bf16[1024,512]{1,0:T(8,128)(2,1)}) %all-gather.6.cloned.1.call-update) | async-done | bytes 1048592 | tf_op jit(solution)/shard_map/all_gather | solution.py:100
  80.5 3.9 %reshape.231 = bf16[2,512,8,64]{3,2,1,0:T(8,128)(2,1)} reshape(bf16[1024,512]{1,0:T(8,128)(2,1)} %all-gather.6.cloned.1.call-done) | data formatting | bytes 2097152 | tf_op jit(solution)/shard_map/reshape;reshape | solution.py:35
  84.4 3.3 %copy.112 = bf16[2,512,8,64]{1,3,2,0:T(8,128)(2,1)} copy(bf16[2,512,8,64]{3,2,1,0:T(8,128)(2,1)} %reshape.231) | data formatting | bytes 2097152
  87.7 45.3 %while.17 = (s32[]{:T(128)}, f32[256,8,3]{0,2,1:T(4,128)S(1)}, f32[256,8,3]{0,2,1:T(4,128)S(1)}, f32[256,8,3,64]{0,3,2,1:T(8,128)}, s32[256]{0:T(256)S(1)}, /*in...) while((s32[]{:T(128)}, f32[256,8,3]{0,2,1:T(4,128)S(1)}, ...), condition=%wide.region_7.8_spmd.clone, body=%wide.region_3.0_spmd.clone.sunk | while | flops 847809280 | bytes 93992664 | solution.py:61
  89.3 6.5 %fusion.61 = (f32[256,8,3]{0,2,1:T(4,128)S(1)}, f32[8,512,256,3]{2,1,3,0:T(8,128)}) fusion(pred[256,512]{0,1:T(8,128)(4,1)S(1)} %compare_and_fusion.2, bf16[256,8,3,64]{0,3,2,1:T(8,128)(2,1)S(1)} %get-tuple-element.402, bf16[2,512,8,64]{1,3,2,0:T(8,128)(2,1)S(1)} %get-tuple-element.401, s32[]{:T(128)} %get-tuple-element.380), kind=kOutput, calls=%fused_computation.4.clone.1 | convolution fusion | flops 412084224 | bytes 14049284 | tf_op jit(solution)/shard_map/while/body/eval_jaxpr/tgrd,bgd->tgrb/dot_general | solution.py:45
  95.8 7.5 %fusion.62 = f32[256,8,3]{0,2,1:T(4,128)S(1)} fusion(f32[8,512,256,3]{2,1,3,0:T(8,128)} %get-tuple-element.363, f32[256,8,3]{0,2,1:T(4,128)S(1)} %select_maximum_fusion.2, pred[256,512]{0,1:T(8,128)(4,1)S(1)} %compare_and_fusion.2), kind=kLoop, calls=%fused_computation.6.clone.1 | loop fusion | flops 15722496 | bytes 12763136 | tf_op jit(solution)/shard_map/while/body/eval_jaxpr/reduce_sum | solution.py:52
  103.4 1.9 copy-done
  105.2 5.5 %bitcast_add_fusion.3 = f32[256,8,3,64]{0,3,2,1:T(8,128)} fusion(f32[256,8,3,64]{0,3,2,1:T(8,128)} %get-tuple-element.383, f32[8,512,256,3]{2,1,3,0:T(8,128)S(1)} %copy-done, f32[256,8,3]{0,2,1:T(4,128)S(1)} %select_maximum_fusion.2, pred[256,512]{0,1:T(8,128)(4,1)S(1)} %compare_and_fusion.2, f32[256,8,3]{0,2,1:T(4,128)S(1)} %get-tuple-element.365, ...), kind=kOutput, calls=%fused_computation.9.clone.1 | convolution fusion | flops 419561472 | bytes 16433665 | tf_op jit(solution)/shard_map/while/body/eval_jaxpr/tgrb,bgd->tgrd/dot_general | solution.py:53
  112.3 6.5 %fusion.61 = (f32[256,8,3]{0,2,1:T(4,128)S(1)}, f32[8,512,256,3]{2,1,3,0:T(8,128)}) fusion(pred[256,512]{0,1:T(8,128)(4,1)S(1)} %compare_and_fusion.2, bf16[256,8,3,64]{0,3,2,1:T(8,128)(2,1)S(1)} %get-tuple-element.402, bf16[2,512,8,64]{1,3,2,0:T(8,128)(2,1)S(1)} %get-tuple-element.401, s32[]{:T(128)} %get-tuple-element.380), kind=kOutput, calls=%fused_computation.4.clone.1 | convolution fusion | flops 412084224 | bytes 14049284 | tf_op jit(solution)/shard_map/while/body/eval_jaxpr/tgrd,bgd->tgrb/dot_general | solution.py:45
  118.8 6.9 %fusion.62 = f32[256,8,3]{0,2,1:T(4,128)S(1)} fusion(f32[8,512,256,3]{2,1,3,0:T(8,128)} %get-tuple-element.363, f32[256,8,3]{0,2,1:T(4,128)S(1)} %select_maximum_fusion.2, pred[256,512]{0,1:T(8,128)(4,1)S(1)} %compare_and_fusion.2), kind=kLoop, calls=%fused_computation.6.clone.1 | loop fusion | flops 15722496 | bytes 12763136 | tf_op jit(solution)/shard_map/while/body/eval_jaxpr/reduce_sum | solution.py:52
  125.8 1.4 copy-done
  127.2 5.8 %bitcast_add_fusion.3 = f32[256,8,3,64]{0,3,2,1:T(8,128)} fusion(f32[256,8,3,64]{0,3,2,1:T(8,128)} %get-tuple-element.383, f32[8,512,256,3]{2,1,3,0:T(8,128)S(1)} %copy-done, f32[256,8,3]{0,2,1:T(4,128)S(1)} %select_maximum_fusion.2, pred[256,512]{0,1:T(8,128)(4,1)S(1)} %compare_and_fusion.2, f32[256,8,3]{0,2,1:T(4,128)S(1)} %get-tuple-element.365, ...), kind=kOutput, calls=%fused_computation.9.clone.1 | convolution fusion | flops 419561472 | bytes 16433665 | tf_op jit(solution)/shard_map/while/body/eval_jaxpr/tgrb,bgd->tgrd/dot_general | solution.py:53
  133.0 2.5 %divide_convert_fusion = bf16[256,8,3,64]{0,3,2,1:T(8,128)(2,1)} fusion(f32[256,8,3,64]{0,3,2,1:T(8,128)} %get-tuple-element.131, f32[256,8,3]{0,2,1:T(4,128)S(1)} %get-tuple-element.132), kind=kLoop, calls=%fused_computation.31 | loop fusion | flops 786432 | bytes 2383872 | tf_op jit(solution)/shard_map/convert_element_type | solution.py:114
  135.5 2.0 %copy.125 = bf16[1,256,8,2,128]{4,3,2,1,0:T(2,128)(2,1)} copy(bf16[1,256,8,2,128]{4,2,3,1,0:T(8,128)(2,1)S(1)} %bitcast.109) | data formatting | bytes 2097152
  137.5 5.8 %all-gather.8.cloned.1.call-done = bf16[1536,1536]{1,0:T(8,128)(2,1)} async-done(((bf16[1536,384]{1,0:T(8,128)(2,1)}), bf16[1536,1536]{1,0:T(8,128)(2,1)}) %all-gather.8.cloned.1.call-update) | async-done | bytes 4718608 | tf_op jit(solution)/shard_map/all_gather | solution.py:175
  143.4 4.1 %fusion.22 = f32[259,1536]{1,0:T(8,128)S(1)} fusion(bf16[1536,1536]{1,0:T(8,128)(2,1)} %all-gather.8.cloned.1.call-done, bf16[3,1536]{0,1:T(8,128)(2,1)S(1)} %constant_dynamic-update-slice_fusion, bf16[256,1536]{0,1:T(8,128)(2,1)} %bitcast.113), kind=kOutput, calls=%fused_computation.32 | convolution fusion | flops 1223706624 | bytes 7105536 | tf_op jit(solution)/shard_map/dot_general | solution.py:173
  147.5 1.2 copy.136
  149.8 29.7 %reduce-scatter.4.cloned.1.call-done = f32[384,3]{1,0:T(8,128)} async-done(((f32[1536,3]{1,0:T(8,128)}), f32[384,3]{1,0:T(8,128)}) %reduce-scatter.4.cloned.1.call-update) | async-done | bytes 4624
  (86 shorter events, 14.5 us)
Async XLA Ops:
  7.2 9.8 %copy-start.8 = (s32[1,3]{1,0:T(1,128)S(1)}, s32[1,3]{1,0:T(1,128)}, u32[]{:S(2)}) copy-start(s32[1,3]{1,0:T(1,128)} %param.18) | copy-start | bytes 40
  7.2 10.3 %copy-start.3 = (bf16[1,3,384]{2,1,0:T(4,128)(2,1)S(1)}, bf16[1,3,384]{2,1,0:T(4,128)(2,1)}, u32[]{:S(2)}) copy-start(bf16[1,3,384]{2,1,0:T(4,128)(2,1)} %param.21) | copy-start | bytes 6916
  7.2 10.4 %copy-start.6 = (bf16[1,3,128]{2,1,0:T(4,128)(2,1)S(1)}, bf16[1,3,128]{2,1,0:T(4,128)(2,1)}, u32[]{:S(2)}) copy-start(bf16[1,3,128]{2,1,0:T(4,128)(2,1)} %param.22) | copy-start | bytes 2308
  7.2 10.4 %copy-start.7 = (bf16[1,3,128]{2,1,0:T(4,128)(2,1)S(1)}, bf16[1,3,128]{2,1,0:T(4,128)(2,1)}, u32[]{:S(2)}) copy-start(bf16[1,3,128]{2,1,0:T(4,128)(2,1)} %param.23) | copy-start | bytes 2308
  7.2 10.6 %copy-start.1 = (bf16[256,1536]{1,0:T(8,128)(2,1)S(1)}, bf16[256,1536]{1,0:T(8,128)(2,1)}, u32[]{:S(2)}) copy-start(bf16[256,1536]{1,0:T(8,128)(2,1)} %param.14) | copy-start | bytes 2359300
  7.2 53.7 %all-gather.4.cloned.1.call-start = ((), (), s32[]{:S(2)}) async-start(), calls=%async_computation.3 | async-start | bytes 1310720 | tf_op jit(solution)/shard_map/all_gather | solution.py:99
  8.0 72.6 %all-gather.6.cloned.1.call-start = ((), (), s32[]{:S(2)}) async-start(), calls=%async_computation.4 | async-start | bytes 1310720 | tf_op jit(solution)/shard_map/all_gather | solution.py:100
  9.8 8.3 %copy-start.5 = (s32[1,128,1]{1,2,0:T(1,128)S(1)}, s32[1,128,1]{1,2,0:T(1,128)}, u32[]{:S(2)}) copy-start(s32[1,128,1]{1,2,0:T(1,128)} %param.19) | copy-start | bytes 1540
  11.8 13.9 %all-to-all-start = ((bf16[256,2,4,128]{0,3,1,2:T(8,128)(2,1)}), bf16[256,2,4,128]{0,3,1,2:T(8,128)(2,1)S(1)}, u32[]{:S(2)}, u32[]{:S(2)}) async-start(bf16[256,2,4,128]{0,3,1,2:T(8,128)(2,1)} %copy.115), calls=%async_computation | async-start | bytes 1048576 | tf_op jit(solution)/shard_map/all_to_all | solution.py:116
  16.2 127.1 %all-gather.8.cloned.1.call-start = ((), (), s32[]{:S(2)}) async-start(), calls=%async_computation.5 | async-start | bytes 5898240 | tf_op jit(solution)/shard_map/all_gather | solution.py:175
  40.8 94.7 %all-to-all-start.1 = ((bf16[256,8,2,128]{3,1,2,0:T(8,128)(2,1)}), bf16[256,8,2,128]{3,1,2,0:T(8,128)(2,1)S(1)}, u32[]{:S(2)}, u32[]{:S(2)}) async-start(bf16[256,8,2,128]{3,1,2,0:T(8,128)(2,1)} %scatter_fusion), calls=%async_computation.1 | async-start | bytes 2097152 | tf_op jit(solution)/shard_map/all_to_all | solution.py:195
  60.6 118.9 %reduce-scatter.4.cloned.1.call-start = ((), (), s32[]{:S(2)}) async-start(), calls=%async_computation.6 | async-start | bytes 983040
  95.8 9.4 %copy-start = (f32[8,512,256,3]{2,1,3,0:T(8,128)S(1)}, f32[8,512,256,3]{2,1,3,0:T(8,128)}, u32[]{:S(2)}) copy-start(f32[8,512,256,3]{2,1,3,0:T(8,128)} %get-tuple-element.363) | copy-start | bytes 37748740 | tf_op jit(solution)/shard_map/while
  118.8 8.4 %copy-start = (f32[8,512,256,3]{2,1,3,0:T(8,128)S(1)}, f32[8,512,256,3]{2,1,3,0:T(8,128)}, u32[]{:S(2)}) copy-start(f32[8,512,256,3]{2,1,3,0:T(8,128)} %get-tuple-element.363) | copy-start | bytes 37748740 | tf_op jit(solution)/shard_map/while
  143.4 5.3 %copy-start.2 = (bf16[256,1536]{1,0:T(8,128)(2,1)S(1)}, bf16[256,1536]{1,0:T(8,128)(2,1)}, u32[]{:S(2)}) copy-start(bf16[256,1536]{1,0:T(8,128)(2,1)} %param.13) | copy-start | bytes 2359300
  147.5 33.1 %copy-start.4 = (bf16[1,3,384]{2,1,0:T(4,128)(2,1)S(1)}, bf16[1,3,384]{2,1,0:T(4,128)(2,1)}, u32[]{:S(2)}) copy-start(bf16[1,3,384]{2,1,0:T(4,128)(2,1)} %param.20) | copy-start | bytes 6916
Sparse Core Ops, SparseCore 0:
  10.2 36.1 all-gather.3
  48.4 32.0 all-gather.5
  82.6 60.6 all-gather.7
  148.8 30.6 reduce-scatter.3
where the time goes:
time: 189 us; the launch traced here: 188 us
  waiting for transfers between devices  57.9 us (31%)
  local copies, waits for them, and re-layouts  40.4 us (21%)
  matrix products  28.8 us (15%)
  starting transfers between devices  24.6 us (13%)
  other arithmetic  20.6 us (11%)
  between operations  14 us (7%)
    unnamed x5, waiting for transfers between devices  31.8 us
    all_to_all x1, starting transfers between devices, shards(): lax.all_to_all(outgoing, 'req', split_axis=0, concat_axis=0, tiled=True)  19.8 us
    reduce_sum x2, other arithmetic, advance(): total = total * factor + jnp.sum(weights, axis=-1)  14.4 us
    all_gather x1, waiting for transfers between devices, shards(): value_portion = lax.all_gather(prompt_values, 'ctx', axis=0, tiled=True)  13.1 us
    dot_general x2, matrix products, advance(): jnp.einsum('tgrd,bgd->tgrb', query_grouped, k_block, preferred_element_ty...  12.9 us
    unnamed x24, local copies, waits for them, and re-layouts  12.6 us
    scatter x1, local copies, waits for them, and re-layouts, shards(): outgoing = jnp.zeros((n_req * lane_cap, PAGE_TOKENS, 2, kv_cols), jnp.bfl...  12.3 us
    dot_general x2, matrix products, advance(): jnp.einsum('tgrb,bgd->tgrd', weights.astype(jnp.bfloat16), v_block, prefe...  11.3 us
  transfers between devices with their start and end apart: 6, of which 4 were waited for; matrix products, arithmetic and copies ran while one was open for 42% of the time, Pallas kernels for 0%

commit v1 on v0

v1 whole, which is shorter than its diff:
```python
import math

import jax
import jax.numpy as jnp
from jax import lax
from jax.experimental import pallas as pl
from jax.experimental.pallas import tpu as pltpu
from jax.sharding import PartitionSpec as P

QUERY_HEADS = 24
KEY_VALUE_HEADS = 8
HEAD_SIZE = 64
PAGE_TOKENS = 8
LONGEST = 512
BLOCK = 256
LANES = 128
DECODE_ROWS = 16

masked_score = -1e30
scale = 1.0 / math.sqrt(HEAD_SIZE)
f32 = jnp.float32
bf16 = jnp.bfloat16


def pair_kernel(k_ref, v_ref, out_ref):
    cols = out_ref.shape[2] // 2
    for c in range(out_ref.shape[0]):
        out_ref[c, :, :cols] = k_ref[:, c * cols : (c + 1) * cols]
        out_ref[c, :, cols:] = v_ref[:, c * cols : (c + 1) * cols]


def split_kernel(place_ref, q_ref, *out_refs):
    n = len(out_refs)
    cols = out_refs[0].shape[1]
    for shift, out_ref in enumerate(out_refs):
        start = pl.multiple_of(lax.rem(place_ref[0] + shift, n) * cols, LANES)
        out_ref[...] = q_ref[:, pl.ds(start, cols)]


def page_kernel(slot_ref, kv_ref, out_ref):
    out_ref[...] = jnp.zeros(out_ref.shape, out_ref.dtype)
    rows = lax.broadcasted_iota(jnp.int32, (2 * LANES, 2 * LANES), 0)
    cols = lax.broadcasted_iota(jnp.int32, (2 * LANES, 2 * LANES), 1)
    weave = (cols == (rows % 2) * LANES + rows // 2).astype(f32).astype(bf16)
    page_rows = 2 * PAGE_TOKENS
    per_chunk = LANES // PAGE_TOKENS
    chunks_per_block = kv_ref.shape[1] // LANES
    for block in range(kv_ref.shape[0]):
        for part in range(chunks_per_block):
            here = pl.ds(part * LANES, LANES)
            both = jnp.concatenate(
                [kv_ref[block, here, :LANES], kv_ref[block, here, LANES:]], axis=0
            )
            woven = jnp.dot(weave, both, preferred_element_type=f32).astype(bf16)
            for p in range(per_chunk):
                page = (block * chunks_per_block + part) * per_chunk + p
                out_ref[slot_ref[page]] = woven[p * page_rows : (p + 1) * page_rows]


def variants(pair, lane):
    wide = pair.astype(f32)
    swapped = pltpu.roll(wide, HEAD_SIZE, 1)
    low = lane < HEAD_SIZE
    zero = jnp.zeros_like(wide)
    return (
        (jnp.where(low, wide, zero), jnp.where(low, zero, swapped)),
        (jnp.where(low, swapped, zero), jnp.where(low, zero, wide)),
    )


def attention_kernel(place_ref, len_ref, *refs):
    n_blocks = (len(refs) - 11) // 2
    q_refs = refs[:n_blocks]
    kv_ref, dq_ref, dk_ref, dv_ref = refs[n_blocks : n_blocks + 4]
    out_refs = refs[n_blocks + 4 : 2 * n_blocks + 4]
    q_ref, out_ref, k_var, v_var, dq_pad, dk_pad, dv_pad = refs[2 * n_blocks + 4 :]
    for pad_ref, given_ref in ((dq_pad, dq_ref), (dk_pad, dk_ref), (dv_pad, dv_ref)):
        pad_ref[...] = jnp.zeros(pad_ref.shape, f32)
        pad_ref[: given_ref.shape[1], :] = given_ref[0].astype(f32)
    place = place_ref[0]
    for shift in range(n_blocks):
        q_ref[lax.rem(place + n_blocks - shift, n_blocks)] = q_refs[shift][...]
    tokens = n_blocks * BLOCK
    end0 = len_ref[0, 0]
    end1 = end0 + len_ref[0, 1]
    heads = q_ref.shape[2] // HEAD_SIZE
    per_kv = QUERY_HEADS // KEY_VALUE_HEADS

    for b in range(n_blocks):
        lane = lax.broadcasted_iota(jnp.int32, (BLOCK, LANES), 1)
        here = pl.ds(b * BLOCK, BLOCK)
        k_all = variants(kv_ref[b, :, :LANES], lane)
        v_all = variants(kv_ref[b, :, LANES:], lane)
        for g in range(2):
            for half in range(2):
                k_var[g, half, here, :] = k_all[g][half].astype(bf16)
                v_var[g, half, here, :] = v_all[g][half].astype(bf16)

    for b in range(n_blocks):
        first = max(0, b - LONGEST // BLOCK)
        keys = (b + 1 - first) * BLOCK
        span = pl.ds(first * BLOCK, keys)
        q_pos = b * BLOCK + lax.broadcasted_iota(jnp.int32, (BLOCK, keys), 0)
        k_pos = first * BLOCK + lax.broadcasted_iota(jnp.int32, (BLOCK, keys), 1)
        begin = jnp.where(q_pos >= end1, end1, jnp.where(q_pos >= end0, end0, 0))
        bias = jnp.where((k_pos <= q_pos) & (k_pos >= begin), 0.0, masked_score).astype(f32)
        lane = lax.broadcasted_iota(jnp.int32, (BLOCK, LANES), 1)
        for pair in range(heads // 2):
            q_pair = q_ref[b, :, pair * LANES : (pair + 1) * LANES] * jnp.asarray(scale, bf16)
            weighted = None
            totals = []
            for half in range(2):
                g = (2 * pair + half) // per_kv
                scores = (
                    lax.dot_general(
                        q_pair, k_var[g, half, span, :], (((1,), (1,)), ((), ())),
                        preferred_element_type=f32,
                    )
                    + bias
                )
                top = jnp.max(scores, axis=1, keepdims=True)
                weights = jnp.exp(scores - top)
                totals.append(jnp.sum(weights, axis=1, keepdims=True))
                part = jnp.dot(
                    weights.astype(bf16), v_var[g, half, span, :], preferred_element_type=f32
                )
                weighted = part if weighted is None else weighted + part
            total = jnp.where(lane < HEAD_SIZE, totals[0], totals[1])
            out_ref[b, :, pair * LANES : (pair + 1) * LANES] = (weighted / total).astype(bf16)

    lane = lax.broadcasted_iota(jnp.int32, (DECODE_ROWS, LANES), 1)
    prompt = lax.broadcasted_iota(jnp.int32, (DECODE_ROWS, tokens), 0)
    token = lax.broadcasted_iota(jnp.int32, (DECODE_ROWS, tokens), 1)
    prompt_of = (token >= end0).astype(jnp.int32) + (token >= end1).astype(jnp.int32)
    bias = jnp.where(prompt == prompt_of, 0.0, masked_score).astype(f32)
    dk_all = variants(dk_pad[...], lane)
    dv_all = variants(dv_pad[...], lane)
    for pair in range(heads // 2):
        q_pair = (dq_pad[:, pair * LANES : (pair + 1) * LANES] * scale).astype(bf16)
        weighted = None
        totals = []
        for half in range(2):
            g = (2 * pair + half) // per_kv
            scores = (
                lax.dot_general(
                    q_pair, k_var[g, half], (((1,), (1,)), ((), ())), preferred_element_type=f32
                )
                + bias
            )
            own = jnp.sum(q_pair.astype(f32) * dk_all[g][half], axis=1, keepdims=True)
            top = jnp.maximum(jnp.max(scores, axis=1, keepdims=True), own)
            weights = jnp.exp(scores - top)
            own_weight = jnp.exp(own - top)
            totals.append(jnp.sum(weights, axis=1, keepdims=True) + own_weight)
            part = (
                jnp.dot(weights.astype(bf16), v_var[g, half], preferred_element_type=f32)
                + own_weight.astype(bf16).astype(f32) * dv_all[g][half]
            )
            weighted = part if weighted is None else weighted + part
        total = jnp.where(lane < HEAD_SIZE, totals[0], totals[1])
        rows = (weighted / total).astype(bf16)
        for result_ref in out_refs:
            result_ref[BLOCK:, pair * LANES : (pair + 1) * LANES] = rows
    for shift, result_ref in enumerate(out_refs):
        result_ref[:BLOCK, :] = out_ref[lax.rem(place + shift, n_blocks)]


def out_kernel(place_ref, core_ref, *refs):
    n = len(refs) - 10
    attn_refs = refs[:n]
    w_ref, beside_ref, across_ref, near_ref, far_ref = refs[n : n + 5]
    res_ref, dres_ref, out_ref, dec_ref, attn_ref = refs[n + 5 :]
    place, core = place_ref[0], core_ref[0]
    width = attn_refs[0].shape[1]
    half = n // 2
    for shift in range(n):
        attn_ref[lax.rem(place + n - shift, n)] = attn_refs[shift][...]

    def project(block, terms):
        start = pl.multiple_of(lax.rem(block, n) * width, LANES)
        total = res_ref[:, pl.ds(start, width)].astype(f32)
        for rows, weight in terms:
            total += jnp.dot(rows, weight, preferred_element_type=f32)
        out_ref[:, pl.ds(start, width)] = total.astype(bf16)

    def whole(ref):
        return [(attn_ref[i, :BLOCK], ref[i * width : (i + 1) * width]) for i in range(n)]

    project(place, whole(w_ref))
    project(place + n - 1 + 2 * core, whole(beside_ref))
    project(place + 1 + 2 * core, whole(across_ref))
    halves = []
    for i in range(half):
        rows = slice(i * width, (i + 1) * width)
        halves.append((attn_ref[core * half + i, :BLOCK], near_ref[rows]))
        halves.append((attn_ref[(1 - core) * half + i, :BLOCK], far_ref[rows]))
    project(place + 2, halves)

    extra = jnp.zeros((DECODE_ROWS, width), f32)
    for i in range(n):
        extra += jnp.dot(
            attn_ref[i, BLOCK:], w_ref[i * width : (i + 1) * width], preferred_element_type=f32
        )
    count = dres_ref.shape[1]
    dec_ref[0] = (dres_ref[0].astype(f32) + extra[:count]).astype(bf16)


def shards(
    prefill_residual,
    prompt_queries,
    prompt_keys,
    prompt_values,
    out_weight,
    prompt_token_counts,
    page_dest,
    decode_residual,
    decoded_queries,
    decoded_keys,
    decoded_values,
):
    n_ctx = lax.axis_size("ctx")
    n_req = lax.axis_size("req")
    rows, width = prompt_queries.shape
    q_cols = width // n_ctx
    kv_cols = prompt_keys.shape[1] // n_ctx
    core = lax.axis_index("req") % 2
    vmem = pl.BlockSpec(memory_space=pltpu.VMEM)
    smem = pl.BlockSpec(memory_space=pltpu.SMEM)

    kv_parts = pl.pallas_call(
        pair_kernel,
        out_shape=jax.ShapeDtypeStruct((n_ctx, rows, 2 * kv_cols), bf16),
        in_specs=[vmem, vmem],
        out_specs=vmem,
        name="pair",
    )(prompt_keys, prompt_values)
    kv = lax.all_to_all(kv_parts, "ctx", 0, 0, tiled=True)
    kv_parts, q_source = lax.optimization_barrier((kv_parts, prompt_queries))
    place = lax.axis_index("ctx").reshape(1)
    send = lambda a, shift: lax.ppermute(a, "ctx", [(i, (i + shift) % n_ctx) for i in range(n_ctx)])
    spread = lambda parts: [parts[0]] + [send(parts[i], i) for i in range(1, n_ctx)]
    q_parts = pl.pallas_call(
        split_kernel,
        out_shape=[jax.ShapeDtypeStruct((rows, q_cols), bf16)] * n_ctx,
        in_specs=[smem, vmem],
        out_specs=[vmem] * n_ctx,
        name="split",
    )(place, q_source)
    q = spread(q_parts)

    pages = page_dest.shape[1]
    dest = page_dest[0, :, 0]
    index = jnp.arange(pages, dtype=jnp.int32)
    lane = jnp.sum(
        ((dest[:, None] == dest[None, :]) & (index[None, :] < index[:, None])).astype(jnp.int32), axis=1
    )
    lane_cap = max(2, 2 * pages // n_req)
    slots, q_parts = lax.optimization_barrier((dest * lane_cap + lane, q_parts))
    outgoing = pl.pallas_call(
        page_kernel,
        out_shape=jax.ShapeDtypeStruct((n_req * lane_cap, 2 * PAGE_TOKENS, kv_cols), bf16),
        in_specs=[smem, vmem],
        out_specs=vmem,
        name="pages",
    )(slots, kv)
    store = lax.all_to_all(outgoing, "req", 0, 0, tiled=True)
    outgoing, w_source, q, kv = lax.optimization_barrier((outgoing, out_weight, q, kv))
    target_page_store = store.reshape(1, n_req * lane_cap, PAGE_TOKENS, 2, kv_cols)

    half_rows = width // 2
    place_of = lambda r, c: r * n_ctx + c % n_ctx
    ring = [
        (place_of(r, c), place_of(r, c + (1 if r % 2 == 0 else -1)))
        for r in range(n_req)
        for c in range(n_ctx)
    ]
    swap = [(r, r ^ 1) for r in range(n_req)]
    w_beside = lax.ppermute(w_source, ("req", "ctx"), ring)

    attention = pl.pallas_call(
        attention_kernel,
        out_shape=[jax.ShapeDtypeStruct((rows + DECODE_ROWS, q_cols), bf16)] * n_ctx,
        in_specs=[smem, smem] + [vmem] * (n_ctx + 4),
        out_specs=[vmem] * n_ctx,
        scratch_shapes=[pltpu.VMEM((n_ctx, rows, q_cols), bf16)] * 2
        + [pltpu.VMEM((2, 2, n_ctx * rows, LANES), bf16)] * 2
        + [pltpu.VMEM((DECODE_ROWS, q_cols), f32)]
        + [pltpu.VMEM((DECODE_ROWS, kv_cols), f32)] * 2,
        name="attend",
    )(place, prompt_token_counts, *q, kv, decoded_queries, decoded_keys, decoded_values)
    back = spread(attention)
    w_beside, attention = lax.optimization_barrier((w_beside, attention))
    w_across = lax.ppermute(w_beside, "req", swap)
    w_near = lax.ppermute(
        lax.dynamic_slice_in_dim(w_beside, core * half_rows, half_rows, 0), ("req", "ctx"), ring
    )
    w_far = lax.ppermute(w_near, "req", swap)

    prefill_out, decode_out = pl.pallas_call(
        out_kernel,
        out_shape=(
            jax.ShapeDtypeStruct(prefill_residual.shape, bf16),
            jax.ShapeDtypeStruct(decode_residual.shape, bf16),
        ),
        in_specs=[smem, smem] + [vmem] * (n_ctx + 7),
        out_specs=(vmem, vmem),
        scratch_shapes=[pltpu.VMEM((n_ctx, rows + DECODE_ROWS, q_cols), bf16)],
        name="project",
    )(
        place,
        core.reshape(1),
        *back,
        out_weight,
        w_beside,
        w_across,
        w_near,
        w_far,
        prefill_residual,
        decode_residual,
    )
    return (prefill_out, target_page_store, decode_out)


def solution(mesh):
    in_specs = (
        P(("req", "ctx"), None),
        P(("req", "ctx"), None),
        P(("req", "ctx"), None),
        P(("req", "ctx"), None),
        P(None, "ctx"),
        P("req", None),
        P("req", None, None),
        P("req", None, "ctx"),
        P("req", None, "ctx"),
        P("req", None, "ctx"),
        P("req", None, "ctx"),
    )
    out_specs = (P(("req", "ctx"), None), P("req", None, None, None, "ctx"), P("req", None, "ctx"))
    return jax.shard_map(shards, mesh=mesh, in_specs=in_specs, out_specs=out_specs, check_vma=False)
```

time: 189 us -> 119 us (0.63)
  the two profiles are of different devices: /device:TPU:4 before, /device:TPU:6 now
where the time goes in v1:
time: 119 us; the launch traced here: 118 us
  starting transfers between devices  52.2 us (44%)
  waiting for transfers between devices  35.9 us (30%)
  Pallas kernels  23.7 us (20%)
  local copies, waits for them, and re-layouts  5.11 us (4%)
    all_to_all x1, starting transfers between devices, shards(): store = lax.all_to_all(outgoing, 'req', 0, 0, tiled=True)  20 us
    ppermute x6, starting transfers between devices, shards(): lax.ppermute(a, 'ctx', [(i, (i + shift) % n_ctx) for i in range(n_ctx)])  18 us
    ppermute x6, waiting for transfers between devices, shards(): lax.ppermute(a, 'ctx', [(i, (i + shift) % n_ctx) for i in range(n_ctx)])  15.7 us
    pallas_call x1, Pallas kernels, shards(): pl.pallas_call(attention_kernel, out_shape=[jax.ShapeDtypeStruct((rows +...  11 us
    ppermute x1, waiting for transfers between devices, shards(): lax.ppermute(lax.dynamic_slice_in_dim(w_beside, core * half_rows, half_ro...  7.42 us
    all_to_all x1, waiting for transfers between devices, shards(): kv = lax.all_to_all(kv_parts, 'ctx', 0, 0, tiled=True)  6.66 us
    ppermute x1, waiting for transfers between devices, shards(): w_beside = lax.ppermute(w_source, ('req', 'ctx'), ring)  6.03 us
    pallas_call x1, Pallas kernels, shards(): pl.pallas_call(out_kernel, out_shape=(jax.ShapeDtypeStruct(prefill_residu...  6.03 us
  transfers between devices with their start and end apart: 12, of which 7 were waited for; matrix products, arithmetic and copies ran while one was open for 1% of the time, Pallas kernels for 16%

profile of v1, /device:TPU:6, one launch (start us, length us, event | category | flops | bytes accessed | tf_op | source)
XLA Modules:
  0.0 118.4 jit_solution(5200067454552019952)
XLA Ops:
  0.6 1.9 %pair.1 = bf16[4,256,256]{2,1,0:T(8,128)(2,1)} custom-call(bf16[256,512]{1,0:T(8,128)(2,1)} %k_ref.1, bf16[256,512]{1,0:T(8,128)(2,1)} %v_ref.1), custom_call_target="tpu_custom_call" | custom-call | tf_op jit(solution)/shard_map/pair/pallas_call | solution.py:230
  2.5 4.6 %all-to-all-start = ((bf16[4,256,256]{2,1,0:T(8,128)(2,1)}), bf16[4,256,256]{2,1,0:T(8,128)(2,1)S(1)}, u32[]{:S(2)}, u32[]{:S(2)}) async-start(bf16[4,256,256]{2,1,0:T(8,128)(2,1)} %pair.1), calls=%async_computation | async-start | bytes 1048576 | tf_op jit(solution)/shard_map/all_to_all | solution.py:237
  7.1 2.1 %split.1 = (bf16[256,384]{1,0:T(8,128)(2,1)}, bf16[256,384]{1,0:T(8,128)(2,1)}, bf16[256,384]{1,0:T(8,128)(2,1)}, bf16[256,384]{1,0:T(8,128)(2,1)}) custom-call(s32[1]{0:T(128)} %bitcast.place_ref, bf16[256,1536]{1,0:T(8,128)(2,1)} %q_ref), custom_call_target="tpu_custom_call" | custom-call | tf_op jit(solution)/shard_map/split/pallas_call | solution.py:242
  10.0 6.7 %all-to-all-done.kv_ref.refs_4_ = bf16[4,256,256]{2,1,0:T(8,128)(2,1)S(1)} async-done(((bf16[4,256,256]{2,1,0:T(8,128)(2,1)}), bf16[4,256,256]{2,1,0:T(8,128)(2,1)S(1)}, u32[]{:S(2)}, u32[]{:S(2)}) %all-to-all-start) | async-done | bytes 524320 | tf_op jit(solution)/shard_map/all_to_all | solution.py:237
  17.4 2.6 %pages.1 = bf16[256,16,128]{2,1,0:T(8,128)(2,1)} custom-call(s32[128]{0:T(128)} %multiply_add_fusion.slot_ref, bf16[4,256,256]{2,1,0:T(8,128)(2,1)} %copy-done), custom_call_target="tpu_custom_call" | custom-call | tf_op jit(solution)/shard_map/pages/pallas_call | solution.py:259
  20.0 20.0 %all-to-all-start.1 = ((bf16[256,16,128]{2,1,0:T(8,128)(2,1)}), bf16[256,16,128]{2,1,0:T(8,128)(2,1)S(1)}, u32[]{:S(2)}, u32[]{:S(2)}) async-start(bf16[256,16,128]{2,1,0:T(8,128)(2,1)} %pages.1), calls=%async_computation.1 | async-start | bytes 2097152 | tf_op jit(solution)/shard_map/all_to_all | solution.py:266
  40.1 2.5 %collective-permute-start = (bf16[256,384]{1,0:T(8,128)(2,1)S(1)}, bf16[256,384]{1,0:T(8,128)(2,1)S(1)}, u32[]{:S(2)}, u32[]{:S(2)}) collective-permute-start(bf16[256,384]{1,0:T(8,128)(2,1)S(1)} %copy-done.17), channel_id=1, source_target_pairs={{0,1},{1,2},{2,3},{3,0},{4,5},{5,6},{6,7},{7,4},{8,9},{9,10},{10,1... | collective-permute-start | bytes 589832 | tf_op jit(solution)/shard_map/ppermute | solution.py:240
  42.6 4.0 %collective-permute-start.1 = (bf16[256,384]{1,0:T(8,128)(2,1)S(1)}, bf16[256,384]{1,0:T(8,128)(2,1)S(1)}, u32[]{:S(2)}, u32[]{:S(2)}) collective-permute-start(bf16[256,384]{1,0:T(8,128)(2,1)S(1)} %copy-done.16), channel_id=1, source_target_pairs={{0,2},{1,3},{2,0},{3,1},{4,6},{5,7},{6,4},{7,5},{8,10},{9,11},{10,... | collective-permute-start | bytes 589832 | tf_op jit(solution)/shard_map/ppermute | solution.py:240
  46.6 2.5 %collective-permute-start.2 = (bf16[256,384]{1,0:T(8,128)(2,1)S(1)}, bf16[256,384]{1,0:T(8,128)(2,1)S(1)}, u32[]{:S(2)}, u32[]{:S(2)}) collective-permute-start(bf16[256,384]{1,0:T(8,128)(2,1)S(1)} %copy-done.15), channel_id=1, source_target_pairs={{0,3},{1,0},{2,1},{3,2},{4,7},{5,4},{6,5},{7,6},{8,11},{9,8},{10,9... | collective-permute-start | bytes 589832 | tf_op jit(solution)/shard_map/ppermute | solution.py:240
  49.1 5.3 %collective-permute-done.refs_1_ = bf16[256,384]{1,0:T(8,128)(2,1)S(1)} collective-permute-done((bf16[256,384]{1,0:T(8,128)(2,1)S(1)}, bf16[256,384]{1,0:T(8,128)(2,1)S(1)}, u32[]{:S(2)}, u32[]{:S(2)}) %collective-permute-start) | collective-permute-done | bytes 196640 | tf_op jit(solution)/shard_map/ppermute | solution.py:240
  55.0 1.8 %collective-permute-done.2.refs_3_ = bf16[256,384]{1,0:T(8,128)(2,1)S(1)} collective-permute-done((bf16[256,384]{1,0:T(8,128)(2,1)S(1)}, bf16[256,384]{1,0:T(8,128)(2,1)S(1)}, u32[]{:S(2)}, u32[]{:S(2)}) %collective-permute-start.2) | collective-permute-done | bytes 196640 | tf_op jit(solution)/shard_map/ppermute | solution.py:240
  57.5 2.2 %collective-permute-start.6 = (bf16[1536,384]{1,0:T(8,128)(2,1)S(1)}, bf16[1536,384]{1,0:T(8,128)(2,1)S(1)}, u32[]{:S(2)}, u32[]{:S(2)}) collective-permute-start(bf16[1536,384]{1,0:T(8,128)(2,1)S(1)} %copy-done.2), channel_id=1, source_target_pairs={{0,1},{1,2},{2,3},{3,0},{4,7},{5,4},{6,5},{7,6},{8,9},{9,10},{10,1... | collective-permute-start | bytes 3538952 | tf_op jit(solution)/shard_map/ppermute | solution.py:278
  59.7 11.0 %attend.1 = (bf16[272,384]{1,0:T(8,128)(2,1)}, bf16[272,384]{1,0:T(8,128)(2,1)}, bf16[272,384]{1,0:T(8,128)(2,1)}, bf16[272,384]{1,0:T(8,128)(2,1)}) custom-call(s32[1]{0:T(128)} %bitcast.place_ref, s32[1,3]{1,0:T(1,128)} %len_ref.1, bf16[256,384]{1,0:T(8,128)(2,1)} %get-tuple-element.28.refs_0_, bf16[256,384]{1,0:T(8,128)(2,1)} %copy-done.9, ...), custom_call_target="tpu_custom_call" | custom-call | tf_op jit(solution)/shard_map/attend/pallas_call | solution.py:280
  70.8 6.0 %collective-permute-done.6.refs_5_ = bf16[1536,384]{1,0:T(8,128)(2,1)S(1)} collective-permute-done((bf16[1536,384]{1,0:T(8,128)(2,1)S(1)}, bf16[1536,384]{1,0:T(8,128)(2,1)S(1)}, u32[]{:S(2)}, u32[]{:S(2)}) %collective-permute-start.6) | collective-permute-done | bytes 1179680 | tf_op jit(solution)/shard_map/ppermute | solution.py:278
  76.9 2.1 %collective-permute-start.8 = (bf16[768,384]{1,0:T(8,128)(2,1)S(1)}, bf16[768,384]{1,0:T(8,128)(2,1)S(1)}, u32[]{:S(2)}, u32[]{:S(2)}) collective-permute-start(bf16[768,384]{1,0:T(8,128)(2,1)S(1)} %constant_dynamic-slice_fusion), channel_id=1, source_target_pairs={{0,1},{1,2},{2,3},{3,0},{4,7},{5,4},{6,5},{7,6},{8,9},{9,10},{10,1... | collective-permute-start | bytes 1769480 | tf_op jit(solution)/shard_map/ppermute | solution.py:294
  79.0 3.5 %collective-permute-start.7 = (bf16[1536,384]{1,0:T(8,128)(2,1)S(1)}, bf16[1536,384]{1,0:T(8,128)(2,1)S(1)}, u32[]{:S(2)}, u32[]{:S(2)}) collective-permute-start(bf16[1536,384]{1,0:T(8,128)(2,1)S(1)} %collective-permute-done.6.refs_5_), channel_id=1, source_target_pairs={{0,4},{4,0},{8,12},{12,8},{16,20},{20,16},{24,28},{28,24},{32,36},... | collective-permute-start | bytes 3538952 | tf_op jit(solution)/shard_map/ppermute | solution.py:293
  82.5 7.4 %collective-permute-done.8.refs_7_ = bf16[768,384]{1,0:T(8,128)(2,1)S(1)} collective-permute-done((bf16[768,384]{1,0:T(8,128)(2,1)S(1)}, bf16[768,384]{1,0:T(8,128)(2,1)S(1)}, u32[]{:S(2)}, u32[]{:S(2)}) %collective-permute-start.8) | collective-permute-done | bytes 589856 | tf_op jit(solution)/shard_map/ppermute | solution.py:294
  89.9 1.9 %collective-permute-start.9 = (bf16[768,384]{1,0:T(8,128)(2,1)S(1)}, bf16[768,384]{1,0:T(8,128)(2,1)S(1)}, u32[]{:S(2)}, u32[]{:S(2)}) collective-permute-start(bf16[768,384]{1,0:T(8,128)(2,1)S(1)} %collective-permute-done.8.refs_7_), channel_id=1, source_target_pairs={{0,4},{4,0},{8,12},{12,8},{16,20},{20,16},{24,28},{28,24},{32,36},... | collective-permute-start | bytes 1769480 | tf_op jit(solution)/shard_map/ppermute | solution.py:297
  91.8 1.9 %collective-permute-start.3 = (bf16[272,384]{1,0:T(8,128)(2,1)S(1)}, bf16[272,384]{1,0:T(8,128)(2,1)S(1)}, u32[]{:S(2)}, u32[]{:S(2)}) collective-permute-start(bf16[272,384]{1,0:T(8,128)(2,1)S(1)} %copy-done.14), channel_id=1, source_target_pairs={{0,1},{1,2},{2,3},{3,0},{4,5},{5,6},{6,7},{7,4},{8,9},{9,10},{10,1... | collective-permute-start | bytes 626696 | tf_op jit(solution)/shard_map/ppermute | solution.py:240
  93.7 4.3 %collective-permute-start.4 = (bf16[272,384]{1,0:T(8,128)(2,1)S(1)}, bf16[272,384]{1,0:T(8,128)(2,1)S(1)}, u32[]{:S(2)}, u32[]{:S(2)}) collective-permute-start(bf16[272,384]{1,0:T(8,128)(2,1)S(1)} %copy-done.13), channel_id=1, source_target_pairs={{0,2},{1,3},{2,0},{3,1},{4,6},{5,7},{6,4},{7,5},{8,10},{9,11},{10,... | collective-permute-start | bytes 626696 | tf_op jit(solution)/shard_map/ppermute | solution.py:240
  98.1 2.7 %collective-permute-start.5 = (bf16[272,384]{1,0:T(8,128)(2,1)S(1)}, bf16[272,384]{1,0:T(8,128)(2,1)S(1)}, u32[]{:S(2)}, u32[]{:S(2)}) collective-permute-start(bf16[272,384]{1,0:T(8,128)(2,1)S(1)} %copy-done.12), channel_id=1, source_target_pairs={{0,3},{1,0},{2,1},{3,2},{4,7},{5,4},{6,5},{7,6},{8,11},{9,8},{10,9... | collective-permute-start | bytes 626696 | tf_op jit(solution)/shard_map/ppermute | solution.py:240
  100.8 6.1 %collective-permute-done.3.refs_1_ = bf16[272,384]{1,0:T(8,128)(2,1)S(1)} collective-permute-done((bf16[272,384]{1,0:T(8,128)(2,1)S(1)}, bf16[272,384]{1,0:T(8,128)(2,1)S(1)}, u32[]{:S(2)}, u32[]{:S(2)}) %collective-permute-start.3) | collective-permute-done | bytes 208928 | tf_op jit(solution)/shard_map/ppermute | solution.py:240
  107.0 2.5 %collective-permute-done.5.refs_3_ = bf16[272,384]{1,0:T(8,128)(2,1)S(1)} collective-permute-done((bf16[272,384]{1,0:T(8,128)(2,1)S(1)}, bf16[272,384]{1,0:T(8,128)(2,1)S(1)}, u32[]{:S(2)}, u32[]{:S(2)}) %collective-permute-start.5) | collective-permute-done | bytes 208928 | tf_op jit(solution)/shard_map/ppermute | solution.py:240
  111.4 6.0 %project.1 = (bf16[256,1536]{1,0:T(8,128)(2,1)}, bf16[1,3,384]{2,1,0:T(4,128)(2,1)}) custom-call(s32[1]{0:T(128)} %bitcast.place_ref, s32[1]{0:T(128)} %bitcast.1.core_ref, bf16[272,384]{1,0:T(8,128)(2,1)} %get-tuple-element.33.refs_0_, bf16[272,384]{1,0:T(8,128)(2,1)} %copy-done.6, bf16[272,384]{1,0:T(8,128)(2,1)} %copy-done.7, bf16[272,384]{1,0:T(8,128)(2,1)} %copy-done.8, ...), custom_call_target="tpu_custom_call" | custom-call | tf_op jit(solution)/shard_map/project/pallas_call | solution.py:299
  (47 shorter events, 5.8 us)
Async XLA Ops:
  2.5 6.7 %copy-start.18 = (s32[1,128,1]{1,2,0:T(1,128)S(1)}, s32[1,128,1]{1,2,0:T(1,128)}, u32[]{:S(2)}) copy-start(s32[1,128,1]{1,2,0:T(1,128)} %param.17) | copy-start | bytes 1540
  2.5 14.1 %all-to-all-start = ((bf16[4,256,256]{2,1,0:T(8,128)(2,1)}), bf16[4,256,256]{2,1,0:T(8,128)(2,1)S(1)}, u32[]{:S(2)}, u32[]{:S(2)}) async-start(bf16[4,256,256]{2,1,0:T(8,128)(2,1)} %pair.1), calls=%async_computation | async-start | bytes 1048576 | tf_op jit(solution)/shard_map/all_to_all | solution.py:237
  20.0 20.1 %copy-start.17 = (bf16[256,384]{1,0:T(8,128)(2,1)S(1)}, bf16[256,384]{1,0:T(8,128)(2,1)}, u32[]{:S(2)}) copy-start(bf16[256,384]{1,0:T(8,128)(2,1)} %get-tuple-element.24) | copy-start | bytes 589828
  20.0 22.6 %copy-start.16 = (bf16[256,384]{1,0:T(8,128)(2,1)S(1)}, bf16[256,384]{1,0:T(8,128)(2,1)}, u32[]{:S(2)}) copy-start(bf16[256,384]{1,0:T(8,128)(2,1)} %get-tuple-element.25) | copy-start | bytes 589828
  20.0 26.5 %copy-start.15 = (bf16[256,384]{1,0:T(8,128)(2,1)S(1)}, bf16[256,384]{1,0:T(8,128)(2,1)}, u32[]{:S(2)}) copy-start(bf16[256,384]{1,0:T(8,128)(2,1)} %get-tuple-element.26) | copy-start | bytes 589828
  20.0 37.5 %copy-start.2 = (bf16[1536,384]{1,0:T(8,128)(2,1)S(1)}, bf16[1536,384]{1,0:T(8,128)(2,1)}, u32[]{:S(2)}) copy-start(bf16[1536,384]{1,0:T(8,128)(2,1)} %refs_4_.1) | copy-start | bytes 3538948
  20.0 97.5 %all-to-all-start.1 = ((bf16[256,16,128]{2,1,0:T(8,128)(2,1)}), bf16[256,16,128]{2,1,0:T(8,128)(2,1)S(1)}, u32[]{:S(2)}, u32[]{:S(2)}) async-start(bf16[256,16,128]{2,1,0:T(8,128)(2,1)} %pages.1), calls=%async_computation.1 | async-start | bytes 2097152 | tf_op jit(solution)/shard_map/all_to_all | solution.py:266
  40.1 14.3 %collective-permute-start = (bf16[256,384]{1,0:T(8,128)(2,1)S(1)}, bf16[256,384]{1,0:T(8,128)(2,1)S(1)}, u32[]{:S(2)}, u32[]{:S(2)}) collective-permute-start(bf16[256,384]{1,0:T(8,128)(2,1)S(1)} %copy-done.17), channel_id=1, source_target_pairs={{0,1},{1,2},{2,3},{3,0},{4,5},{5,6},{6,7},{7,4},{8,9},{9,10},{10,1... | collective-permute-start | bytes 589832 | tf_op jit(solution)/shard_map/ppermute | solution.py:240
  42.6 11.8 %collective-permute-start.1 = (bf16[256,384]{1,0:T(8,128)(2,1)S(1)}, bf16[256,384]{1,0:T(8,128)(2,1)S(1)}, u32[]{:S(2)}, u32[]{:S(2)}) collective-permute-start(bf16[256,384]{1,0:T(8,128)(2,1)S(1)} %copy-done.16), channel_id=1, source_target_pairs={{0,2},{1,3},{2,0},{3,1},{4,6},{5,7},{6,4},{7,5},{8,10},{9,11},{10,... | collective-permute-start | bytes 589832 | tf_op jit(solution)/shard_map/ppermute | solution.py:240
  46.6 10.3 %collective-permute-start.2 = (bf16[256,384]{1,0:T(8,128)(2,1)S(1)}, bf16[256,384]{1,0:T(8,128)(2,1)S(1)}, u32[]{:S(2)}, u32[]{:S(2)}) collective-permute-start(bf16[256,384]{1,0:T(8,128)(2,1)S(1)} %copy-done.15), channel_id=1, source_target_pairs={{0,3},{1,0},{2,1},{3,2},{4,7},{5,4},{6,5},{7,6},{8,11},{9,8},{10,9... | collective-permute-start | bytes 589832 | tf_op jit(solution)/shard_map/ppermute | solution.py:240
  57.5 19.3 %collective-permute-start.6 = (bf16[1536,384]{1,0:T(8,128)(2,1)S(1)}, bf16[1536,384]{1,0:T(8,128)(2,1)S(1)}, u32[]{:S(2)}, u32[]{:S(2)}) collective-permute-start(bf16[1536,384]{1,0:T(8,128)(2,1)S(1)} %copy-done.2), channel_id=1, source_target_pairs={{0,1},{1,2},{2,3},{3,0},{4,7},{5,4},{6,5},{7,6},{8,9},{9,10},{10,1... | collective-permute-start | bytes 3538952 | tf_op jit(solution)/shard_map/ppermute | solution.py:278
  70.8 21.0 %copy-start.14 = (bf16[272,384]{1,0:T(8,128)(2,1)S(1)}, bf16[272,384]{1,0:T(8,128)(2,1)}, u32[]{:S(2)}) copy-start(bf16[272,384]{1,0:T(8,128)(2,1)} %get-tuple-element.34) | copy-start | bytes 626692
  70.8 23.0 %copy-start.13 = (bf16[272,384]{1,0:T(8,128)(2,1)S(1)}, bf16[272,384]{1,0:T(8,128)(2,1)}, u32[]{:S(2)}) copy-start(bf16[272,384]{1,0:T(8,128)(2,1)} %get-tuple-element.35) | copy-start | bytes 626692
  70.8 27.3 %copy-start.12 = (bf16[272,384]{1,0:T(8,128)(2,1)S(1)}, bf16[272,384]{1,0:T(8,128)(2,1)}, u32[]{:S(2)}) copy-start(bf16[272,384]{1,0:T(8,128)(2,1)} %get-tuple-element.36) | copy-start | bytes 626692
  76.8 33.6 %copy-start.1 = (bf16[1536,384]{1,0:T(8,128)(2,1)}, bf16[1536,384]{1,0:T(8,128)(2,1)S(1)}, u32[]{:S(2)}) copy-start(bf16[1536,384]{1,0:T(8,128)(2,1)S(1)} %collective-permute-done.6.refs_5_) | copy-start | bytes 3538948
  76.9 13.0 %collective-permute-start.8 = (bf16[768,384]{1,0:T(8,128)(2,1)S(1)}, bf16[768,384]{1,0:T(8,128)(2,1)S(1)}, u32[]{:S(2)}, u32[]{:S(2)}) collective-permute-start(bf16[768,384]{1,0:T(8,128)(2,1)S(1)} %constant_dynamic-slice_fusion), channel_id=1, source_target_pairs={{0,1},{1,2},{2,3},{3,0},{4,7},{5,4},{6,5},{7,6},{8,9},{9,10},{10,1... | collective-permute-start | bytes 1769480 | tf_op jit(solution)/shard_map/ppermute | solution.py:294
  79.0 30.5 %collective-permute-start.7 = (bf16[1536,384]{1,0:T(8,128)(2,1)S(1)}, bf16[1536,384]{1,0:T(8,128)(2,1)S(1)}, u32[]{:S(2)}, u32[]{:S(2)}) collective-permute-start(bf16[1536,384]{1,0:T(8,128)(2,1)S(1)} %collective-permute-done.6.refs_5_), channel_id=1, source_target_pairs={{0,4},{4,0},{8,12},{12,8},{16,20},{20,16},{24,28},{28,24},{32,36},... | collective-permute-start | bytes 3538952 | tf_op jit(solution)/shard_map/ppermute | solution.py:293
  89.9 19.6 %copy-start.4 = (bf16[768,384]{1,0:T(8,128)(2,1)}, bf16[768,384]{1,0:T(8,128)(2,1)S(1)}, u32[]{:S(2)}) copy-start(bf16[768,384]{1,0:T(8,128)(2,1)S(1)} %collective-permute-done.8.refs_7_) | copy-start | bytes 1769476
  89.9 19.6 %collective-permute-start.9 = (bf16[768,384]{1,0:T(8,128)(2,1)S(1)}, bf16[768,384]{1,0:T(8,128)(2,1)S(1)}, u32[]{:S(2)}, u32[]{:S(2)}) collective-permute-start(bf16[768,384]{1,0:T(8,128)(2,1)S(1)} %collective-permute-done.8.refs_7_), channel_id=1, source_target_pairs={{0,4},{4,0},{8,12},{12,8},{16,20},{20,16},{24,28},{28,24},{32,36},... | collective-permute-start | bytes 1769480 | tf_op jit(solution)/shard_map/ppermute | solution.py:297
  91.8 15.1 %collective-permute-start.3 = (bf16[272,384]{1,0:T(8,128)(2,1)S(1)}, bf16[272,384]{1,0:T(8,128)(2,1)S(1)}, u32[]{:S(2)}, u32[]{:S(2)}) collective-permute-start(bf16[272,384]{1,0:T(8,128)(2,1)S(1)} %copy-done.14), channel_id=1, source_target_pairs={{0,1},{1,2},{2,3},{3,0},{4,5},{5,6},{6,7},{7,4},{8,9},{9,10},{10,1... | collective-permute-start | bytes 626696 | tf_op jit(solution)/shard_map/ppermute | solution.py:240
  93.7 13.2 %collective-permute-start.4 = (bf16[272,384]{1,0:T(8,128)(2,1)S(1)}, bf16[272,384]{1,0:T(8,128)(2,1)S(1)}, u32[]{:S(2)}, u32[]{:S(2)}) collective-permute-start(bf16[272,384]{1,0:T(8,128)(2,1)S(1)} %copy-done.13), channel_id=1, source_target_pairs={{0,2},{1,3},{2,0},{3,1},{4,6},{5,7},{6,4},{7,5},{8,10},{9,11},{10,... | collective-permute-start | bytes 626696 | tf_op jit(solution)/shard_map/ppermute | solution.py:240
  98.1 11.4 %collective-permute-start.5 = (bf16[272,384]{1,0:T(8,128)(2,1)S(1)}, bf16[272,384]{1,0:T(8,128)(2,1)S(1)}, u32[]{:S(2)}, u32[]{:S(2)}) collective-permute-start(bf16[272,384]{1,0:T(8,128)(2,1)S(1)} %copy-done.12), channel_id=1, source_target_pairs={{0,3},{1,0},{2,1},{3,2},{4,7},{5,4},{6,5},{7,6},{8,11},{9,8},{10,9... | collective-permute-start | bytes 626696 | tf_op jit(solution)/shard_map/ppermute | solution.py:240
  107.0 2.6 %copy-start.6 = (bf16[272,384]{1,0:T(8,128)(2,1)}, bf16[272,384]{1,0:T(8,128)(2,1)S(1)}, u32[]{:S(2)}) copy-start(bf16[272,384]{1,0:T(8,128)(2,1)S(1)} %collective-permute-done.3.refs_1_) | copy-start | bytes 626692
  107.0 2.6 %copy-start.7 = (bf16[272,384]{1,0:T(8,128)(2,1)}, bf16[272,384]{1,0:T(8,128)(2,1)S(1)}, u32[]{:S(2)}) copy-start(bf16[272,384]{1,0:T(8,128)(2,1)S(1)} %collective-permute-done.4.refs_2_) | copy-start | bytes 626692
  (7 other events, 6.6 us)

commit v2 on v1

--- a/solution.py
+++ b/solution.py
@@ -166,43 +166,46 @@
 
 
 def out_kernel(place_ref, core_ref, *refs):
-    n = len(refs) - 10
+    n = len(refs) - 13
     attn_refs = refs[:n]
-    w_ref, beside_ref, across_ref, near_ref, far_ref = refs[n : n + 5]
-    res_ref, dres_ref, out_ref, dec_ref, attn_ref = refs[n + 5 :]
+    w_refs = refs[n : n + 4]
+    res_hbm, dres_ref, out_ref, dec_ref, attn_ref, w_all, res_ref, w_sems, res_sem = refs[n + 4 :]
     place, core = place_ref[0], core_ref[0]
     width = attn_refs[0].shape[1]
-    half = n // 2
+    fetches = [
+        pltpu.make_async_copy(w_ref, w_all.at[i], w_sems.at[i]) for i, w_ref in enumerate(w_refs)
+    ]
+    residual = pltpu.make_async_copy(res_hbm, res_ref, res_sem)
+    fetches[0].start()
+    residual.start()
+    for fetch in fetches[1:]:
+        fetch.start()
     for shift in range(n):
         attn_ref[lax.rem(place + n - shift, n)] = attn_refs[shift][...]
-
-    def project(block, terms):
+    blocks = (place, place + n - 1 + 2 * core, place + 1 + 2 * core, place + 2)
+    for i, block in enumerate(blocks):
+        fetches[i].wait()
+        if i == 0:
+            residual.wait()
         start = pl.multiple_of(lax.rem(block, n) * width, LANES)
         total = res_ref[:, pl.ds(start, width)].astype(f32)
-        for rows, weight in terms:
-            total += jnp.dot(rows, weight, preferred_element_type=f32)
+        for h in range(n):
+            total += jnp.dot(
+                attn_ref[h, :BLOCK],
+                w_all[i, h * width : (h + 1) * width, :],
+                preferred_element_type=f32,
+            )
         out_ref[:, pl.ds(start, width)] = total.astype(bf16)
-
-    def whole(ref):
-        return [(attn_ref[i, :BLOCK], ref[i * width : (i + 1) * width]) for i in range(n)]
-
-    project(place, whole(w_ref))
-    project(place + n - 1 + 2 * core, whole(beside_ref))
-    project(place + 1 + 2 * core, whole(across_ref))
-    halves = []
-    for i in range(half):
-        rows = slice(i * width, (i + 1) * width)
-        halves.append((attn_ref[core * half + i, :BLOCK], near_ref[rows]))
-        halves.append((attn_ref[(1 - core) * half + i, :BLOCK], far_ref[rows]))
-    project(place + 2, halves)
-
-    extra = jnp.zeros((DECODE_ROWS, width), f32)
-    for i in range(n):
-        extra += jnp.dot(
-            attn_ref[i, BLOCK:], w_ref[i * width : (i + 1) * width], preferred_element_type=f32
-        )
-    count = dres_ref.shape[1]
-    dec_ref[0] = (dres_ref[0].astype(f32) + extra[:count]).astype(bf16)
+        if i == 0:
+            extra = jnp.zeros((DECODE_ROWS, width), f32)
+            for h in range(n):
+                extra += jnp.dot(
+                    attn_ref[h, BLOCK:],
+                    w_all[0, h * width : (h + 1) * width, :],
+                    preferred_element_type=f32,
+                )
+            count = dres_ref.shape[1]
+            dec_ref[0] = (dres_ref[0].astype(f32) + extra[:count]).astype(bf16)
 
 
 def shards(
@@ -226,6 +229,8 @@
     core = lax.axis_index("req") % 2
     vmem = pl.BlockSpec(memory_space=pltpu.VMEM)
     smem = pl.BlockSpec(memory_space=pltpu.SMEM)
+    anywhere = pl.BlockSpec(memory_space=pl.ANY)
+    near = lambda a: pltpu.with_memory_space_constraint(a, pltpu.VMEM)
 
     kv_parts = pl.pallas_call(
         pair_kernel,
@@ -235,7 +240,7 @@
         name="pair",
     )(prompt_keys, prompt_values)
     kv = lax.all_to_all(kv_parts, "ctx", 0, 0, tiled=True)
-    kv_parts, q_source = lax.optimization_barrier((kv_parts, prompt_queries))
+    kv_parts, q_source, w_source = lax.optimization_barrier((kv_parts, prompt_queries, out_weight))
     place = lax.axis_index("ctx").reshape(1)
     send = lambda a, shift: lax.ppermute(a, "ctx", [(i, (i + shift) % n_ctx) for i in range(n_ctx)])
     spread = lambda parts: [parts[0]] + [send(parts[i], i) for i in range(1, n_ctx)]
@@ -246,7 +251,14 @@
         out_specs=[vmem] * n_ctx,
         name="split",
     )(place, q_source)
-    q = spread(q_parts)
+
+    place_of = lambda r, c: r * n_ctx + c % n_ctx
+    ring = [
+        (place_of(r, c), place_of(r, c + (1 if r % 2 == 0 else -1)))
+        for r in range(n_req)
+        for c in range(n_ctx)
+    ]
+    swap = [(r, r ^ 1) for r in range(n_req)]
 
     pages = page_dest.shape[1]
     dest = page_dest[0, :, 0]
@@ -262,20 +274,16 @@
         in_specs=[smem, vmem],
         out_specs=vmem,
         name="pages",
-    )(slots, kv)
+    )(slots, near(kv))
     store = lax.all_to_all(outgoing, "req", 0, 0, tiled=True)
-    outgoing, w_source, q, kv = lax.optimization_barrier((outgoing, out_weight, q, kv))
+    w_beside = lax.ppermute(w_source, ("req", "ctx"), ring)
+    outgoing, w_beside = lax.optimization_barrier((outgoing, w_beside))
+    w_beside, q_parts = lax.optimization_barrier((w_beside, q_parts))
+    q = spread(q_parts)
     target_page_store = store.reshape(1, n_req * lane_cap, PAGE_TOKENS, 2, kv_cols)
 
-    half_rows = width // 2
-    place_of = lambda r, c: r * n_ctx + c % n_ctx
-    ring = [
-        (place_of(r, c), place_of(r, c + (1 if r % 2 == 0 else -1)))
-        for r in range(n_req)
-        for c in range(n_ctx)
-    ]
-    swap = [(r, r ^ 1) for r in range(n_req)]
-    w_beside = lax.ppermute(w_source, ("req", "ctx"), ring)
+    w_across = lax.ppermute(w_beside, "req", swap)
+    w_beyond = lax.ppermute(w_beside, ("req", "ctx"), ring)
 
     attention = pl.pallas_call(
         attention_kernel,
@@ -287,34 +295,34 @@
         + [pltpu.VMEM((DECODE_ROWS, q_cols), f32)]
         + [pltpu.VMEM((DECODE_ROWS, kv_cols), f32)] * 2,
         name="attend",
-    )(place, prompt_token_counts, *q, kv, decoded_queries, decoded_keys, decoded_values)
+        cost_estimate=pl.CostEstimate(flops=30000000000, transcendentals=0, bytes_accessed=0),
+    )(place, prompt_token_counts, q[0], *map(near, q[1:]), near(kv), decoded_queries, decoded_keys, decoded_values)
     back = spread(attention)
-    w_beside, attention = lax.optimization_barrier((w_beside, attention))
-    w_across = lax.ppermute(w_beside, "req", swap)
-    w_near = lax.ppermute(
-        lax.dynamic_slice_in_dim(w_beside, core * half_rows, half_rows, 0), ("req", "ctx"), ring
-    )
-    w_far = lax.ppermute(w_near, "req", swap)
-
     prefill_out, decode_out = pl.pallas_call(
         out_kernel,
         out_shape=(
             jax.ShapeDtypeStruct(prefill_residual.shape, bf16),
             jax.ShapeDtypeStruct(decode_residual.shape, bf16),
         ),
-        in_specs=[smem, smem] + [vmem] * (n_ctx + 7),
+        in_specs=[smem, smem] + [vmem] * n_ctx + [anywhere] * 5 + [vmem],
         out_specs=(vmem, vmem),
-        scratch_shapes=[pltpu.VMEM((n_ctx, rows + DECODE_ROWS, q_cols), bf16)],
+        scratch_shapes=[
+            pltpu.VMEM((n_ctx, rows + DECODE_ROWS, q_cols), bf16),
+            pltpu.VMEM((n_ctx, width, q_cols), bf16),
+            pltpu.VMEM((rows, width), bf16),
+            pltpu.SemaphoreType.DMA((n_ctx,)),
+            pltpu.SemaphoreType.DMA,
+        ],
         name="project",
     )(
         place,
         core.reshape(1),
-        *back,
+        back[0],
+        *map(near, back[1:]),
         out_weight,
         w_beside,
         w_across,
-        w_near,
-        w_far,
+        w_beyond,
         prefill_residual,
         decode_residual,
     )

time: 119 us -> 96.6 us (0.81)
  the two profiles are of different devices: /device:TPU:6 before, /device:TPU:10 now
where the time goes in v2:
time: 96.6 us; the launch traced here: 96 us
  starting transfers between devices  52.1 us (54%)
  Pallas kernels  24.2 us (25%)
  waiting for transfers between devices  16.1 us (17%)
  local copies, waits for them, and re-layouts  2.02 us (2%)
    ppermute x6, starting transfers between devices, shards(): lax.ppermute(a, 'ctx', [(i, (i + shift) % n_ctx) for i in range(n_ctx)])  20.3 us
    all_to_all x1, starting transfers between devices, shards(): store = lax.all_to_all(outgoing, 'req', 0, 0, tiled=True)  19.7 us
    pallas_call x1, Pallas kernels, shards(): pl.pallas_call(attention_kernel, out_shape=[jax.ShapeDtypeStruct((rows +...  10.5 us
    ppermute x6, waiting for transfers between devices, shards(): lax.ppermute(a, 'ctx', [(i, (i + shift) % n_ctx) for i in range(n_ctx)])  9.49 us
    pallas_call x1, Pallas kernels, shards(): pl.pallas_call(out_kernel, out_shape=(jax.ShapeDtypeStruct(prefill_residu...  7.42 us
    all_to_all x1, starting transfers between devices, shards(): kv = lax.all_to_all(kv_parts, 'ctx', 0, 0, tiled=True)  4.91 us
    ppermute x1, starting transfers between devices, shards(): w_beside = lax.ppermute(w_source, ('req', 'ctx'), ring)  3.36 us
    all_to_all x1, waiting for transfers between devices, shards(): kv = lax.all_to_all(kv_parts, 'ctx', 0, 0, tiled=True)  3.32 us
  transfers between devices with their start and end apart: 11, of which 5 were waited for; matrix products, arithmetic and copies ran while one was open for 1% of the time, Pallas kernels for 23%

profile of v2, /device:TPU:10, one launch (start us, length us, event | category | flops | bytes accessed | tf_op | source)
XLA Modules:
  0.0 96.0 jit_solution(2825381379755416686)
XLA Ops:
  0.7 2.0 %pair.1 = bf16[4,256,256]{2,1,0:T(8,128)(2,1)} custom-call(bf16[256,512]{1,0:T(8,128)(2,1)} %k_ref.1, bf16[256,512]{1,0:T(8,128)(2,1)} %v_ref.1), custom_call_target="tpu_custom_call" | custom-call | tf_op jit(solution)/shard_map/pair/pallas_call | solution.py:235
  2.7 4.9 %all-to-all-start = ((bf16[4,256,256]{2,1,0:T(8,128)(2,1)}), bf16[4,256,256]{2,1,0:T(8,128)(2,1)S(1)}, u32[]{:S(2)}, u32[]{:S(2)}) async-start(bf16[4,256,256]{2,1,0:T(8,128)(2,1)} %pair.1), calls=%async_computation | async-start | bytes 1048576 | tf_op jit(solution)/shard_map/all_to_all | solution.py:242
  7.6 3.4 %collective-permute-start = (bf16[1536,384]{1,0:T(8,128)(2,1)S(1)}, bf16[1536,384]{1,0:T(8,128)(2,1)}, u32[]{:S(2)}, u32[]{:S(2)}) collective-permute-start(bf16[1536,384]{1,0:T(8,128)(2,1)S(1)} %copy-done), channel_id=1, source_target_pairs={{0,1},{1,2},{2,3},{3,0},{4,7},{5,4},{6,5},{7,6},{8,9},{9,10},{10,1... | collective-permute-start | bytes 3538952 | tf_op jit(solution)/shard_map/ppermute | solution.py:279
  11.1 2.1 %split.1 = (bf16[256,384]{1,0:T(8,128)(2,1)}, bf16[256,384]{1,0:T(8,128)(2,1)}, bf16[256,384]{1,0:T(8,128)(2,1)}, bf16[256,384]{1,0:T(8,128)(2,1)}) custom-call(s32[1]{0:T(128)} %bitcast.place_ref, bf16[256,1536]{1,0:T(8,128)(2,1)} %q_ref), custom_call_target="tpu_custom_call" | custom-call | tf_op jit(solution)/shard_map/split/pallas_call | solution.py:247
  13.2 0.5 multiply_add_fusion.slot_ref
  13.7 3.3 %all-to-all-done.kv_ref.refs_4_ = bf16[4,256,256]{2,1,0:T(8,128)(2,1)S(1)} async-done(((bf16[4,256,256]{2,1,0:T(8,128)(2,1)}), bf16[4,256,256]{2,1,0:T(8,128)(2,1)S(1)}, u32[]{:S(2)}, u32[]{:S(2)}) %all-to-all-start) | async-done | bytes 524320 | tf_op jit(solution)/shard_map/all_to_all | solution.py:242
  17.1 2.2 %pages.1 = bf16[256,16,128]{2,1,0:T(8,128)(2,1)} custom-call(s32[128]{0:T(128)} %multiply_add_fusion.slot_ref, bf16[4,256,256]{2,1,0:T(8,128)(2,1)S(1)} %all-to-all-done.kv_ref.refs_4_), custom_call_target="tpu_custom_call" | custom-call | tf_op jit(solution)/shard_map/pages/pallas_call | solution.py:271
  19.2 19.7 %all-to-all-start.1 = ((bf16[256,16,128]{2,1,0:T(8,128)(2,1)}), bf16[256,16,128]{2,1,0:T(8,128)(2,1)S(1)}, u32[]{:S(2)}, u32[]{:S(2)}) async-start(bf16[256,16,128]{2,1,0:T(8,128)(2,1)} %pages.1), calls=%async_computation.1 | async-start | bytes 2097152 | tf_op jit(solution)/shard_map/all_to_all | solution.py:278
  38.9 1.9 %collective-permute-start.1 = (bf16[256,384]{1,0:T(8,128)(2,1)}, bf16[256,384]{1,0:T(8,128)(2,1)S(1)}, u32[]{:S(2)}, u32[]{:S(2)}) collective-permute-start(bf16[256,384]{1,0:T(8,128)(2,1)} %get-tuple-element.39), channel_id=1, source_target_pairs={{0,1},{1,2},{2,3},{3,0},{4,5},{5,6},{6,7},{7,4},{8,9},{9,10},{10,1... | collective-permute-start | bytes 589832 | tf_op jit(solution)/shard_map/ppermute | solution.py:245
  40.9 4.0 %collective-permute-start.2 = (bf16[256,384]{1,0:T(8,128)(2,1)}, bf16[256,384]{1,0:T(8,128)(2,1)S(1)}, u32[]{:S(2)}, u32[]{:S(2)}) collective-permute-start(bf16[256,384]{1,0:T(8,128)(2,1)} %get-tuple-element.40), channel_id=1, source_target_pairs={{0,2},{1,3},{2,0},{3,1},{4,6},{5,7},{6,4},{7,5},{8,10},{9,11},{10,... | collective-permute-start | bytes 589832 | tf_op jit(solution)/shard_map/ppermute | solution.py:245
  44.9 3.9 %collective-permute-start.3 = (bf16[256,384]{1,0:T(8,128)(2,1)S(1)}, bf16[256,384]{1,0:T(8,128)(2,1)S(1)}, u32[]{:S(2)}, u32[]{:S(2)}) collective-permute-start(bf16[256,384]{1,0:T(8,128)(2,1)S(1)} %copy-done.2), channel_id=1, source_target_pairs={{0,3},{1,0},{2,1},{3,2},{4,7},{5,4},{6,5},{7,6},{8,11},{9,8},{10,9... | collective-permute-start | bytes 589832 | tf_op jit(solution)/shard_map/ppermute | solution.py:245
  48.8 2.0 %collective-permute-start.8 = (bf16[1536,384]{1,0:T(8,128)(2,1)}, bf16[1536,384]{1,0:T(8,128)(2,1)S(1)}, u32[]{:S(2)}, u32[]{:S(2)}) collective-permute-start(bf16[1536,384]{1,0:T(8,128)(2,1)} %collective-permute-done.refs_5_), channel_id=1, source_target_pairs={{0,1},{1,2},{2,3},{3,0},{4,7},{5,4},{6,5},{7,6},{8,9},{9,10},{10,1... | collective-permute-start | bytes 3538952 | tf_op jit(solution)/shard_map/ppermute | solution.py:286
  50.7 1.9 %collective-permute-start.7 = (bf16[1536,384]{1,0:T(8,128)(2,1)}, bf16[1536,384]{1,0:T(8,128)(2,1)}, u32[]{:S(2)}, u32[]{:S(2)}) collective-permute-start(bf16[1536,384]{1,0:T(8,128)(2,1)} %collective-permute-done.refs_5_), channel_id=1, source_target_pairs={{0,4},{4,0},{8,12},{12,8},{16,20},{20,16},{24,28},{28,24},{32,36},... | collective-permute-start | bytes 3538952 | tf_op jit(solution)/shard_map/ppermute | solution.py:285
  52.7 3.0 %collective-permute-done.3.refs_3_ = bf16[256,384]{1,0:T(8,128)(2,1)S(1)} collective-permute-done((bf16[256,384]{1,0:T(8,128)(2,1)S(1)}, bf16[256,384]{1,0:T(8,128)(2,1)S(1)}, u32[]{:S(2)}, u32[]{:S(2)}) %collective-permute-start.3) | collective-permute-done | bytes 196640 | tf_op jit(solution)/shard_map/ppermute | solution.py:245
  55.7 10.5 %attend.1 = (bf16[272,384]{1,0:T(8,128)(2,1)}, bf16[272,384]{1,0:T(8,128)(2,1)}, bf16[272,384]{1,0:T(8,128)(2,1)}, bf16[272,384]{1,0:T(8,128)(2,1)}) custom-call(s32[1]{0:T(128)} %bitcast.place_ref, s32[1,3]{1,0:T(1,128)} %len_ref.1, bf16[256,384]{1,0:T(8,128)(2,1)} %get-tuple-element.38.refs_0_, bf16[256,384]{1,0:T(8,128)(2,1)S(1)} %collective-permute-done.1.refs_1_, ...), custom_call_target="tpu_custom_call" | custom-call | flops 30000001024 | tf_op jit(solution)/shard_map/attend/pallas_call | solution.py:288
  66.2 3.2 %collective-permute-start.4 = (bf16[272,384]{1,0:T(8,128)(2,1)}, bf16[272,384]{1,0:T(8,128)(2,1)S(1)}, u32[]{:S(2)}, u32[]{:S(2)}) collective-permute-start(bf16[272,384]{1,0:T(8,128)(2,1)} %get-tuple-element.43), channel_id=1, source_target_pairs={{0,1},{1,2},{2,3},{3,0},{4,5},{5,6},{6,7},{7,4},{8,9},{9,10},{10,1... | collective-permute-start | bytes 626696 | tf_op jit(solution)/shard_map/ppermute | solution.py:245
  69.4 3.7 %collective-permute-start.5 = (bf16[272,384]{1,0:T(8,128)(2,1)}, bf16[272,384]{1,0:T(8,128)(2,1)S(1)}, u32[]{:S(2)}, u32[]{:S(2)}) collective-permute-start(bf16[272,384]{1,0:T(8,128)(2,1)} %get-tuple-element.44), channel_id=1, source_target_pairs={{0,2},{1,3},{2,0},{3,1},{4,6},{5,7},{6,4},{7,5},{8,10},{9,11},{10,... | collective-permute-start | bytes 626696 | tf_op jit(solution)/shard_map/ppermute | solution.py:245
  73.1 3.7 %collective-permute-start.6 = (bf16[272,384]{1,0:T(8,128)(2,1)}, bf16[272,384]{1,0:T(8,128)(2,1)S(1)}, u32[]{:S(2)}, u32[]{:S(2)}) collective-permute-start(bf16[272,384]{1,0:T(8,128)(2,1)} %get-tuple-element.45), channel_id=1, source_target_pairs={{0,3},{1,0},{2,1},{3,2},{4,7},{5,4},{6,5},{7,6},{8,11},{9,8},{10,9... | collective-permute-start | bytes 626696 | tf_op jit(solution)/shard_map/ppermute | solution.py:245
  76.8 3.9 %collective-permute-done.5.refs_2_ = bf16[272,384]{1,0:T(8,128)(2,1)S(1)} collective-permute-done((bf16[272,384]{1,0:T(8,128)(2,1)}, bf16[272,384]{1,0:T(8,128)(2,1)S(1)}, u32[]{:S(2)}, u32[]{:S(2)}) %collective-permute-start.5) | collective-permute-done | bytes 208928 | tf_op jit(solution)/shard_map/ppermute | solution.py:245
  80.7 2.5 %collective-permute-done.6.refs_3_ = bf16[272,384]{1,0:T(8,128)(2,1)S(1)} collective-permute-done((bf16[272,384]{1,0:T(8,128)(2,1)}, bf16[272,384]{1,0:T(8,128)(2,1)S(1)}, u32[]{:S(2)}, u32[]{:S(2)}) %collective-permute-start.6) | collective-permute-done | bytes 208928 | tf_op jit(solution)/shard_map/ppermute | solution.py:245
  83.2 1.0 %copy-done.1 = bf16[1536,384]{1,0:T(8,128)(2,1)} copy-done((bf16[1536,384]{1,0:T(8,128)(2,1)}, bf16[1536,384]{1,0:T(8,128)(2,1)S(1)}, u32[]{:S(2)}) %copy-start.1) | copy-done | bytes 1179672
  84.3 7.4 %project.1 = (bf16[256,1536]{1,0:T(8,128)(2,1)}, bf16[1,3,384]{2,1,0:T(4,128)(2,1)}) custom-call(s32[1]{0:T(128)} %bitcast.place_ref, s32[1]{0:T(128)} %bitcast.1.core_ref, bf16[272,384]{1,0:T(8,128)(2,1)} %get-tuple-element.42.refs_0_, bf16[272,384]{1,0:T(8,128)(2,1)S(1)} %collective-permute-done.4.refs_1_, ...), custom_call_target="tpu_custom_call" | custom-call | tf_op jit(solution)/shard_map/project/pallas_call | solution.py:301
  91.7 3.3 %all-to-all-done.1 = bf16[256,16,128]{2,1,0:T(8,128)(2,1)S(1)} async-done(((bf16[256,16,128]{2,1,0:T(8,128)(2,1)}), bf16[256,16,128]{2,1,0:T(8,128)(2,1)S(1)}, u32[]{:S(2)}, u32[]{:S(2)}) %all-to-all-start.1) | async-done | bytes 1048608 | tf_op jit(solution)/shard_map/all_to_all | solution.py:278
  95.0 1.0 %copy.15 = bf16[1,256,8,2,128]{4,3,2,1,0:T(2,128)(2,1)} copy(bf16[1,256,8,2,128]{4,3,2,1,0:T(2,128)(2,1)S(1)} %bitcast.5) | data formatting | bytes 2097152
  (14 shorter events, 0.2 us)
Async XLA Ops:
  0.6 6.9 %copy-start = (bf16[1536,384]{1,0:T(8,128)(2,1)S(1)}, bf16[1536,384]{1,0:T(8,128)(2,1)}, u32[]{:S(2)}) copy-start(bf16[1536,384]{1,0:T(8,128)(2,1)} %refs_4_.1) | copy-start | bytes 3538948
  0.6 10.3 %copy-start.3 = (s32[1,128,1]{1,2,0:T(1,128)S(1)}, s32[1,128,1]{1,2,0:T(1,128)}, u32[]{:S(2)}) copy-start(s32[1,128,1]{1,2,0:T(1,128)} %param.17) | copy-start | bytes 1540
  2.7 14.4 %all-to-all-start = ((bf16[4,256,256]{2,1,0:T(8,128)(2,1)}), bf16[4,256,256]{2,1,0:T(8,128)(2,1)S(1)}, u32[]{:S(2)}, u32[]{:S(2)}) async-start(bf16[4,256,256]{2,1,0:T(8,128)(2,1)} %pair.1), calls=%async_computation | async-start | bytes 1048576 | tf_op jit(solution)/shard_map/all_to_all | solution.py:242
  7.6 31.3 %collective-permute-start = (bf16[1536,384]{1,0:T(8,128)(2,1)S(1)}, bf16[1536,384]{1,0:T(8,128)(2,1)}, u32[]{:S(2)}, u32[]{:S(2)}) collective-permute-start(bf16[1536,384]{1,0:T(8,128)(2,1)S(1)} %copy-done), channel_id=1, source_target_pairs={{0,1},{1,2},{2,3},{3,0},{4,7},{5,4},{6,5},{7,6},{8,9},{9,10},{10,1... | collective-permute-start | bytes 3538952 | tf_op jit(solution)/shard_map/ppermute | solution.py:279
  19.2 25.6 %copy-start.2 = (bf16[256,384]{1,0:T(8,128)(2,1)S(1)}, bf16[256,384]{1,0:T(8,128)(2,1)}, u32[]{:S(2)}) copy-start(bf16[256,384]{1,0:T(8,128)(2,1)} %get-tuple-element.41) | copy-start | bytes 589828
  19.2 75.8 %all-to-all-start.1 = ((bf16[256,16,128]{2,1,0:T(8,128)(2,1)}), bf16[256,16,128]{2,1,0:T(8,128)(2,1)S(1)}, u32[]{:S(2)}, u32[]{:S(2)}) async-start(bf16[256,16,128]{2,1,0:T(8,128)(2,1)} %pages.1), calls=%async_computation.1 | async-start | bytes 2097152 | tf_op jit(solution)/shard_map/all_to_all | solution.py:278
  38.9 13.8 %collective-permute-start.1 = (bf16[256,384]{1,0:T(8,128)(2,1)}, bf16[256,384]{1,0:T(8,128)(2,1)S(1)}, u32[]{:S(2)}, u32[]{:S(2)}) collective-permute-start(bf16[256,384]{1,0:T(8,128)(2,1)} %get-tuple-element.39), channel_id=1, source_target_pairs={{0,1},{1,2},{2,3},{3,0},{4,5},{5,6},{6,7},{7,4},{8,9},{9,10},{10,1... | collective-permute-start | bytes 589832 | tf_op jit(solution)/shard_map/ppermute | solution.py:245
  40.9 11.8 %collective-permute-start.2 = (bf16[256,384]{1,0:T(8,128)(2,1)}, bf16[256,384]{1,0:T(8,128)(2,1)S(1)}, u32[]{:S(2)}, u32[]{:S(2)}) collective-permute-start(bf16[256,384]{1,0:T(8,128)(2,1)} %get-tuple-element.40), channel_id=1, source_target_pairs={{0,2},{1,3},{2,0},{3,1},{4,6},{5,7},{6,4},{7,5},{8,10},{9,11},{10,... | collective-permute-start | bytes 589832 | tf_op jit(solution)/shard_map/ppermute | solution.py:245
  44.9 10.8 %collective-permute-start.3 = (bf16[256,384]{1,0:T(8,128)(2,1)S(1)}, bf16[256,384]{1,0:T(8,128)(2,1)S(1)}, u32[]{:S(2)}, u32[]{:S(2)}) collective-permute-start(bf16[256,384]{1,0:T(8,128)(2,1)S(1)} %copy-done.2), channel_id=1, source_target_pairs={{0,3},{1,0},{2,1},{3,2},{4,7},{5,4},{6,5},{7,6},{8,11},{9,8},{10,9... | collective-permute-start | bytes 589832 | tf_op jit(solution)/shard_map/ppermute | solution.py:245
  48.8 34.5 %collective-permute-start.8 = (bf16[1536,384]{1,0:T(8,128)(2,1)}, bf16[1536,384]{1,0:T(8,128)(2,1)S(1)}, u32[]{:S(2)}, u32[]{:S(2)}) collective-permute-start(bf16[1536,384]{1,0:T(8,128)(2,1)} %collective-permute-done.refs_5_), channel_id=1, source_target_pairs={{0,1},{1,2},{2,3},{3,0},{4,7},{5,4},{6,5},{7,6},{8,9},{9,10},{10,1... | collective-permute-start | bytes 3538952 | tf_op jit(solution)/shard_map/ppermute | solution.py:286
  50.7 32.5 %collective-permute-start.7 = (bf16[1536,384]{1,0:T(8,128)(2,1)}, bf16[1536,384]{1,0:T(8,128)(2,1)}, u32[]{:S(2)}, u32[]{:S(2)}) collective-permute-start(bf16[1536,384]{1,0:T(8,128)(2,1)} %collective-permute-done.refs_5_), channel_id=1, source_target_pairs={{0,4},{4,0},{8,12},{12,8},{16,20},{20,16},{24,28},{28,24},{32,36},... | collective-permute-start | bytes 3538952 | tf_op jit(solution)/shard_map/ppermute | solution.py:285
  66.2 10.5 %collective-permute-start.4 = (bf16[272,384]{1,0:T(8,128)(2,1)}, bf16[272,384]{1,0:T(8,128)(2,1)S(1)}, u32[]{:S(2)}, u32[]{:S(2)}) collective-permute-start(bf16[272,384]{1,0:T(8,128)(2,1)} %get-tuple-element.43), channel_id=1, source_target_pairs={{0,1},{1,2},{2,3},{3,0},{4,5},{5,6},{6,7},{7,4},{8,9},{9,10},{10,1... | collective-permute-start | bytes 626696 | tf_op jit(solution)/shard_map/ppermute | solution.py:245
  69.4 11.3 %collective-permute-start.5 = (bf16[272,384]{1,0:T(8,128)(2,1)}, bf16[272,384]{1,0:T(8,128)(2,1)S(1)}, u32[]{:S(2)}, u32[]{:S(2)}) collective-permute-start(bf16[272,384]{1,0:T(8,128)(2,1)} %get-tuple-element.44), channel_id=1, source_target_pairs={{0,2},{1,3},{2,0},{3,1},{4,6},{5,7},{6,4},{7,5},{8,10},{9,11},{10,... | collective-permute-start | bytes 626696 | tf_op jit(solution)/shard_map/ppermute | solution.py:245
  73.1 10.1 %collective-permute-start.6 = (bf16[272,384]{1,0:T(8,128)(2,1)}, bf16[272,384]{1,0:T(8,128)(2,1)S(1)}, u32[]{:S(2)}, u32[]{:S(2)}) collective-permute-start(bf16[272,384]{1,0:T(8,128)(2,1)} %get-tuple-element.45), channel_id=1, source_target_pairs={{0,3},{1,0},{2,1},{3,2},{4,7},{5,4},{6,5},{7,6},{8,11},{9,8},{10,9... | collective-permute-start | bytes 626696 | tf_op jit(solution)/shard_map/ppermute | solution.py:245
  83.2 1.0 %copy-start.1 = (bf16[1536,384]{1,0:T(8,128)(2,1)}, bf16[1536,384]{1,0:T(8,128)(2,1)S(1)}, u32[]{:S(2)}) copy-start(bf16[1536,384]{1,0:T(8,128)(2,1)S(1)} %collective-permute-done.8.refs_7_) | copy-start | bytes 3538948

commit v3 on v2

--- a/solution.py
+++ b/solution.py
@@ -166,46 +166,30 @@
 
 
 def out_kernel(place_ref, core_ref, *refs):
-    n = len(refs) - 13
-    attn_refs = refs[:n]
-    w_refs = refs[n : n + 4]
-    res_hbm, dres_ref, out_ref, dec_ref, attn_ref, w_all, res_ref, w_sems, res_sem = refs[n + 4 :]
+    n = len(refs) - 9
+    attn_refs, w_refs = refs[:n], refs[n : n + 4]
+    res_ref, dres_ref, out_ref, dec_ref, attn_ref = refs[n + 4 :]
     place, core = place_ref[0], core_ref[0]
     width = attn_refs[0].shape[1]
-    fetches = [
-        pltpu.make_async_copy(w_ref, w_all.at[i], w_sems.at[i]) for i, w_ref in enumerate(w_refs)
-    ]
-    residual = pltpu.make_async_copy(res_hbm, res_ref, res_sem)
-    fetches[0].start()
-    residual.start()
-    for fetch in fetches[1:]:
-        fetch.start()
     for shift in range(n):
         attn_ref[lax.rem(place + n - shift, n)] = attn_refs[shift][...]
+
+    def times(rows, w_ref):
+        total = None
+        for h in range(n):
+            weight = w_ref[h * width : (h + 1) * width, :]
+            part = jnp.dot(attn_ref[h, rows], weight, preferred_element_type=f32)
+            total = part if total is None else total + part
+        return total
+
     blocks = (place, place + n - 1 + 2 * core, place + 1 + 2 * core, place + 2)
-    for i, block in enumerate(blocks):
-        fetches[i].wait()
-        if i == 0:
-            residual.wait()
+    for w_ref, block in zip(w_refs, blocks):
         start = pl.multiple_of(lax.rem(block, n) * width, LANES)
-        total = res_ref[:, pl.ds(start, width)].astype(f32)
-        for h in range(n):
-            total += jnp.dot(
-                attn_ref[h, :BLOCK],
-                w_all[i, h * width : (h + 1) * width, :],
-                preferred_element_type=f32,
-            )
-        out_ref[:, pl.ds(start, width)] = total.astype(bf16)
-        if i == 0:
-            extra = jnp.zeros((DECODE_ROWS, width), f32)
-            for h in range(n):
-                extra += jnp.dot(
-                    attn_ref[h, BLOCK:],
-                    w_all[0, h * width : (h + 1) * width, :],
-                    preferred_element_type=f32,
-                )
-            count = dres_ref.shape[1]
-            dec_ref[0] = (dres_ref[0].astype(f32) + extra[:count]).astype(bf16)
+        residual = res_ref[:, pl.ds(start, width)].astype(f32)
+        out_ref[:, pl.ds(start, width)] = (residual + times(slice(0, BLOCK), w_ref)).astype(bf16)
+    count = dres_ref.shape[1]
+    extra = times(slice(BLOCK, BLOCK + DECODE_ROWS), w_refs[0])
+    dec_ref[0] = (dres_ref[0].astype(f32) + extra[:count]).astype(bf16)
 
 
 def shards(
@@ -229,7 +213,6 @@
     core = lax.axis_index("req") % 2
     vmem = pl.BlockSpec(memory_space=pltpu.VMEM)
     smem = pl.BlockSpec(memory_space=pltpu.SMEM)
-    anywhere = pl.BlockSpec(memory_space=pl.ANY)
     near = lambda a: pltpu.with_memory_space_constraint(a, pltpu.VMEM)
 
     kv_parts = pl.pallas_call(
@@ -304,14 +287,10 @@
             jax.ShapeDtypeStruct(prefill_residual.shape, bf16),
             jax.ShapeDtypeStruct(decode_residual.shape, bf16),
         ),
-        in_specs=[smem, smem] + [vmem] * n_ctx + [anywhere] * 5 + [vmem],
+        in_specs=[smem, smem] + [vmem] * (n_ctx + 6),
         out_specs=(vmem, vmem),
         scratch_shapes=[
             pltpu.VMEM((n_ctx, rows + DECODE_ROWS, q_cols), bf16),
-            pltpu.VMEM((n_ctx, width, q_cols), bf16),
-            pltpu.VMEM((rows, width), bf16),
-            pltpu.SemaphoreType.DMA((n_ctx,)),
-            pltpu.SemaphoreType.DMA,
         ],
         name="project",
     )(

time: 96.6 us -> 96.6 us (level)
  waiting for transfers between devices: 16.1 us -> 17.9 us
  Pallas kernels: 24.2 us -> 22.6 us
    all_to_all x1, waiting for transfers between devices: 3.31 us -> 4.93 us  [shards(): store = lax.all_to_all(outgoing, 'req', 0, 0, tiled=True)]
    pallas_call x1, Pallas kernels: 7.42 us -> 5.8 us  [shards(): pl.pallas_call(out_kernel, out_shape=(jax.ShapeDtypeStruct(prefill_residu...]
  transfers between devices with their start and end apart: 11 -> 11, of which waited for: 5 -> 5; matrix products, arithmetic and copies ran while one was open for 1% -> 1% of each run, Pallas kernels for 23% -> 21%
where the time goes in v3:
time: 96.6 us; the launch traced here: 96 us
  starting transfers between devices  51.9 us (54%)
  Pallas kernels  22.6 us (23%)
  waiting for transfers between devices  17.9 us (19%)
  local copies, waits for them, and re-layouts  2.02 us (2%)
    ppermute x6, starting transfers between devices, shards(): lax.ppermute(a, 'ctx', [(i, (i + shift) % n_ctx) for i in range(n_ctx)])  20.1 us
    all_to_all x1, starting transfers between devices, shards(): store = lax.all_to_all(outgoing, 'req', 0, 0, tiled=True)  19.7 us
    pallas_call x1, Pallas kernels, shards(): pl.pallas_call(attention_kernel, out_shape=[jax.ShapeDtypeStruct((rows +...  10.5 us
    ppermute x6, waiting for transfers between devices, shards(): lax.ppermute(a, 'ctx', [(i, (i + shift) % n_ctx) for i in range(n_ctx)])  9.67 us
    pallas_call x1, Pallas kernels, shards(): pl.pallas_call(out_kernel, out_shape=(jax.ShapeDtypeStruct(prefill_residu...  5.8 us
    all_to_all x1, waiting for transfers between devices, shards(): store = lax.all_to_all(outgoing, 'req', 0, 0, tiled=True)  4.93 us
    all_to_all x1, starting transfers between devices, shards(): kv = lax.all_to_all(kv_parts, 'ctx', 0, 0, tiled=True)  4.91 us
    ppermute x1, starting transfers between devices, shards(): w_beside = lax.ppermute(w_source, ('req', 'ctx'), ring)  3.36 us
  transfers between devices with their start and end apart: 11, of which 5 were waited for; matrix products, arithmetic and copies ran while one was open for 1% of the time, Pallas kernels for 21%

profile of v3, /device:TPU:10, one launch (start us, length us, event | category | flops | bytes accessed | tf_op | source)
XLA Modules:
  0.0 96.0 jit_solution(12576156751851249023)
XLA Ops:
  0.7 2.0 %pair.1 = bf16[4,256,256]{2,1,0:T(8,128)(2,1)} custom-call(bf16[256,512]{1,0:T(8,128)(2,1)} %k_ref.1, bf16[256,512]{1,0:T(8,128)(2,1)} %v_ref.1), custom_call_target="tpu_custom_call" | custom-call | tf_op jit(solution)/shard_map/pair/pallas_call | solution.py:218
  2.7 4.9 %all-to-all-start = ((bf16[4,256,256]{2,1,0:T(8,128)(2,1)}), bf16[4,256,256]{2,1,0:T(8,128)(2,1)S(1)}, u32[]{:S(2)}, u32[]{:S(2)}) async-start(bf16[4,256,256]{2,1,0:T(8,128)(2,1)} %pair.1), calls=%async_computation | async-start | bytes 1048576 | tf_op jit(solution)/shard_map/all_to_all | solution.py:225
  7.6 3.4 %collective-permute-start = (bf16[1536,384]{1,0:T(8,128)(2,1)S(1)}, bf16[1536,384]{1,0:T(8,128)(2,1)}, u32[]{:S(2)}, u32[]{:S(2)}) collective-permute-start(bf16[1536,384]{1,0:T(8,128)(2,1)S(1)} %copy-done), channel_id=1, source_target_pairs={{0,1},{1,2},{2,3},{3,0},{4,7},{5,4},{6,5},{7,6},{8,9},{9,10},{10,1... | collective-permute-start | bytes 3538952 | tf_op jit(solution)/shard_map/ppermute | solution.py:262
  11.1 2.1 %split.1 = (bf16[256,384]{1,0:T(8,128)(2,1)}, bf16[256,384]{1,0:T(8,128)(2,1)}, bf16[256,384]{1,0:T(8,128)(2,1)}, bf16[256,384]{1,0:T(8,128)(2,1)}) custom-call(s32[1]{0:T(128)} %bitcast.place_ref, bf16[256,1536]{1,0:T(8,128)(2,1)} %q_ref), custom_call_target="tpu_custom_call" | custom-call | tf_op jit(solution)/shard_map/split/pallas_call | solution.py:230
  13.2 0.5 multiply_add_fusion.slot_ref
  13.7 3.3 %all-to-all-done.kv_ref.refs_4_ = bf16[4,256,256]{2,1,0:T(8,128)(2,1)S(1)} async-done(((bf16[4,256,256]{2,1,0:T(8,128)(2,1)}), bf16[4,256,256]{2,1,0:T(8,128)(2,1)S(1)}, u32[]{:S(2)}, u32[]{:S(2)}) %all-to-all-start) | async-done | bytes 524320 | tf_op jit(solution)/shard_map/all_to_all | solution.py:225
  17.1 2.2 %pages.1 = bf16[256,16,128]{2,1,0:T(8,128)(2,1)} custom-call(s32[128]{0:T(128)} %multiply_add_fusion.slot_ref, bf16[4,256,256]{2,1,0:T(8,128)(2,1)S(1)} %all-to-all-done.kv_ref.refs_4_), custom_call_target="tpu_custom_call" | custom-call | tf_op jit(solution)/shard_map/pages/pallas_call | solution.py:254
  19.3 19.7 %all-to-all-start.1 = ((bf16[256,16,128]{2,1,0:T(8,128)(2,1)}), bf16[256,16,128]{2,1,0:T(8,128)(2,1)S(1)}, u32[]{:S(2)}, u32[]{:S(2)}) async-start(bf16[256,16,128]{2,1,0:T(8,128)(2,1)} %pages.1), calls=%async_computation.1 | async-start | bytes 2097152 | tf_op jit(solution)/shard_map/all_to_all | solution.py:261
  38.9 1.9 %collective-permute-start.1 = (bf16[256,384]{1,0:T(8,128)(2,1)}, bf16[256,384]{1,0:T(8,128)(2,1)S(1)}, u32[]{:S(2)}, u32[]{:S(2)}) collective-permute-start(bf16[256,384]{1,0:T(8,128)(2,1)} %get-tuple-element.39), channel_id=1, source_target_pairs={{0,1},{1,2},{2,3},{3,0},{4,5},{5,6},{6,7},{7,4},{8,9},{9,10},{10,1... | collective-permute-start | bytes 589832 | tf_op jit(solution)/shard_map/ppermute | solution.py:228
  40.9 4.0 %collective-permute-start.2 = (bf16[256,384]{1,0:T(8,128)(2,1)}, bf16[256,384]{1,0:T(8,128)(2,1)S(1)}, u32[]{:S(2)}, u32[]{:S(2)}) collective-permute-start(bf16[256,384]{1,0:T(8,128)(2,1)} %get-tuple-element.40), channel_id=1, source_target_pairs={{0,2},{1,3},{2,0},{3,1},{4,6},{5,7},{6,4},{7,5},{8,10},{9,11},{10,... | collective-permute-start | bytes 589832 | tf_op jit(solution)/shard_map/ppermute | solution.py:228
  44.9 3.9 %collective-permute-start.3 = (bf16[256,384]{1,0:T(8,128)(2,1)S(1)}, bf16[256,384]{1,0:T(8,128)(2,1)S(1)}, u32[]{:S(2)}, u32[]{:S(2)}) collective-permute-start(bf16[256,384]{1,0:T(8,128)(2,1)S(1)} %copy-done.2), channel_id=1, source_target_pairs={{0,3},{1,0},{2,1},{3,2},{4,7},{5,4},{6,5},{7,6},{8,11},{9,8},{10,9... | collective-permute-start | bytes 589832 | tf_op jit(solution)/shard_map/ppermute | solution.py:228
  48.8 2.0 %collective-permute-start.8 = (bf16[1536,384]{1,0:T(8,128)(2,1)}, bf16[1536,384]{1,0:T(8,128)(2,1)S(1)}, u32[]{:S(2)}, u32[]{:S(2)}) collective-permute-start(bf16[1536,384]{1,0:T(8,128)(2,1)} %collective-permute-done.refs_5_), channel_id=1, source_target_pairs={{0,1},{1,2},{2,3},{3,0},{4,7},{5,4},{6,5},{7,6},{8,9},{9,10},{10,1... | collective-permute-start | bytes 3538952 | tf_op jit(solution)/shard_map/ppermute | solution.py:269
  50.7 1.9 %collective-permute-start.7 = (bf16[1536,384]{1,0:T(8,128)(2,1)}, bf16[1536,384]{1,0:T(8,128)(2,1)}, u32[]{:S(2)}, u32[]{:S(2)}) collective-permute-start(bf16[1536,384]{1,0:T(8,128)(2,1)} %collective-permute-done.refs_5_), channel_id=1, source_target_pairs={{0,4},{4,0},{8,12},{12,8},{16,20},{20,16},{24,28},{28,24},{32,36},... | collective-permute-start | bytes 3538952 | tf_op jit(solution)/shard_map/ppermute | solution.py:268
  52.7 3.0 %collective-permute-done.3.refs_3_ = bf16[256,384]{1,0:T(8,128)(2,1)S(1)} collective-permute-done((bf16[256,384]{1,0:T(8,128)(2,1)S(1)}, bf16[256,384]{1,0:T(8,128)(2,1)S(1)}, u32[]{:S(2)}, u32[]{:S(2)}) %collective-permute-start.3) | collective-permute-done | bytes 196640 | tf_op jit(solution)/shard_map/ppermute | solution.py:228
  55.7 10.5 %attend.1 = (bf16[272,384]{1,0:T(8,128)(2,1)}, bf16[272,384]{1,0:T(8,128)(2,1)}, bf16[272,384]{1,0:T(8,128)(2,1)}, bf16[272,384]{1,0:T(8,128)(2,1)}) custom-call(s32[1]{0:T(128)} %bitcast.place_ref, s32[1,3]{1,0:T(1,128)} %len_ref.1, bf16[256,384]{1,0:T(8,128)(2,1)} %get-tuple-element.38.refs_0_, bf16[256,384]{1,0:T(8,128)(2,1)S(1)} %collective-permute-done.1.refs_1_, ...), custom_call_target="tpu_custom_call" | custom-call | flops 30000001024 | tf_op jit(solution)/shard_map/attend/pallas_call | solution.py:271
  66.2 3.2 %collective-permute-start.4 = (bf16[272,384]{1,0:T(8,128)(2,1)}, bf16[272,384]{1,0:T(8,128)(2,1)S(1)}, u32[]{:S(2)}, u32[]{:S(2)}) collective-permute-start(bf16[272,384]{1,0:T(8,128)(2,1)} %get-tuple-element.43), channel_id=1, source_target_pairs={{0,1},{1,2},{2,3},{3,0},{4,5},{5,6},{6,7},{7,4},{8,9},{9,10},{10,1... | collective-permute-start | bytes 626696 | tf_op jit(solution)/shard_map/ppermute | solution.py:228
  69.4 3.7 %collective-permute-start.5 = (bf16[272,384]{1,0:T(8,128)(2,1)}, bf16[272,384]{1,0:T(8,128)(2,1)S(1)}, u32[]{:S(2)}, u32[]{:S(2)}) collective-permute-start(bf16[272,384]{1,0:T(8,128)(2,1)} %get-tuple-element.44), channel_id=1, source_target_pairs={{0,2},{1,3},{2,0},{3,1},{4,6},{5,7},{6,4},{7,5},{8,10},{9,11},{10,... | collective-permute-start | bytes 626696 | tf_op jit(solution)/shard_map/ppermute | solution.py:228
  73.1 3.5 %collective-permute-start.6 = (bf16[272,384]{1,0:T(8,128)(2,1)}, bf16[272,384]{1,0:T(8,128)(2,1)S(1)}, u32[]{:S(2)}, u32[]{:S(2)}) collective-permute-start(bf16[272,384]{1,0:T(8,128)(2,1)} %get-tuple-element.45), channel_id=1, source_target_pairs={{0,3},{1,0},{2,1},{3,2},{4,7},{5,4},{6,5},{7,6},{8,11},{9,8},{10,9... | collective-permute-start | bytes 626696 | tf_op jit(solution)/shard_map/ppermute | solution.py:228
  76.6 4.1 %collective-permute-done.5.refs_2_ = bf16[272,384]{1,0:T(8,128)(2,1)S(1)} collective-permute-done((bf16[272,384]{1,0:T(8,128)(2,1)}, bf16[272,384]{1,0:T(8,128)(2,1)S(1)}, u32[]{:S(2)}, u32[]{:S(2)}) %collective-permute-start.5) | collective-permute-done | bytes 208928 | tf_op jit(solution)/shard_map/ppermute | solution.py:228
  80.7 2.5 %collective-permute-done.6.refs_3_ = bf16[272,384]{1,0:T(8,128)(2,1)S(1)} collective-permute-done((bf16[272,384]{1,0:T(8,128)(2,1)}, bf16[272,384]{1,0:T(8,128)(2,1)S(1)}, u32[]{:S(2)}, u32[]{:S(2)}) %collective-permute-start.6) | collective-permute-done | bytes 208928 | tf_op jit(solution)/shard_map/ppermute | solution.py:228
  83.3 1.0 %copy-done.1 = bf16[1536,384]{1,0:T(8,128)(2,1)} copy-done((bf16[1536,384]{1,0:T(8,128)(2,1)}, bf16[1536,384]{1,0:T(8,128)(2,1)S(1)}, u32[]{:S(2)}) %copy-start.1) | copy-done | bytes 1179672
  84.3 5.8 %project.1 = (bf16[256,1536]{1,0:T(8,128)(2,1)}, bf16[1,3,384]{2,1,0:T(4,128)(2,1)}) custom-call(s32[1]{0:T(128)} %bitcast.place_ref, s32[1]{0:T(128)} %bitcast.1.core_ref, bf16[272,384]{1,0:T(8,128)(2,1)} %get-tuple-element.42.refs_0_, bf16[272,384]{1,0:T(8,128)(2,1)S(1)} %collective-permute-done.4.refs_1_, ...), custom_call_target="tpu_custom_call" | custom-call | tf_op jit(solution)/shard_map/project/pallas_call | solution.py:284
  90.1 4.9 %all-to-all-done.1 = bf16[256,16,128]{2,1,0:T(8,128)(2,1)S(1)} async-done(((bf16[256,16,128]{2,1,0:T(8,128)(2,1)}), bf16[256,16,128]{2,1,0:T(8,128)(2,1)S(1)}, u32[]{:S(2)}, u32[]{:S(2)}) %all-to-all-start.1) | async-done | bytes 1048608 | tf_op jit(solution)/shard_map/all_to_all | solution.py:261
  95.0 1.0 %copy.15 = bf16[1,256,8,2,128]{4,3,2,1,0:T(2,128)(2,1)} copy(bf16[1,256,8,2,128]{4,3,2,1,0:T(2,128)(2,1)S(1)} %bitcast.5) | data formatting | bytes 2097152
  (14 shorter events, 0.2 us)
Async XLA Ops:
  0.6 6.9 %copy-start = (bf16[1536,384]{1,0:T(8,128)(2,1)S(1)}, bf16[1536,384]{1,0:T(8,128)(2,1)}, u32[]{:S(2)}) copy-start(bf16[1536,384]{1,0:T(8,128)(2,1)} %refs_4_.1) | copy-start | bytes 3538948
  0.6 10.3 %copy-start.3 = (s32[1,128,1]{1,2,0:T(1,128)S(1)}, s32[1,128,1]{1,2,0:T(1,128)}, u32[]{:S(2)}) copy-start(s32[1,128,1]{1,2,0:T(1,128)} %param.17) | copy-start | bytes 1540
  2.7 14.4 %all-to-all-start = ((bf16[4,256,256]{2,1,0:T(8,128)(2,1)}), bf16[4,256,256]{2,1,0:T(8,128)(2,1)S(1)}, u32[]{:S(2)}, u32[]{:S(2)}) async-start(bf16[4,256,256]{2,1,0:T(8,128)(2,1)} %pair.1), calls=%async_computation | async-start | bytes 1048576 | tf_op jit(solution)/shard_map/all_to_all | solution.py:225
  7.6 31.3 %collective-permute-start = (bf16[1536,384]{1,0:T(8,128)(2,1)S(1)}, bf16[1536,384]{1,0:T(8,128)(2,1)}, u32[]{:S(2)}, u32[]{:S(2)}) collective-permute-start(bf16[1536,384]{1,0:T(8,128)(2,1)S(1)} %copy-done), channel_id=1, source_target_pairs={{0,1},{1,2},{2,3},{3,0},{4,7},{5,4},{6,5},{7,6},{8,9},{9,10},{10,1... | collective-permute-start | bytes 3538952 | tf_op jit(solution)/shard_map/ppermute | solution.py:262
  19.2 25.6 %copy-start.2 = (bf16[256,384]{1,0:T(8,128)(2,1)S(1)}, bf16[256,384]{1,0:T(8,128)(2,1)}, u32[]{:S(2)}) copy-start(bf16[256,384]{1,0:T(8,128)(2,1)} %get-tuple-element.41) | copy-start | bytes 589828
  19.3 75.8 %all-to-all-start.1 = ((bf16[256,16,128]{2,1,0:T(8,128)(2,1)}), bf16[256,16,128]{2,1,0:T(8,128)(2,1)S(1)}, u32[]{:S(2)}, u32[]{:S(2)}) async-start(bf16[256,16,128]{2,1,0:T(8,128)(2,1)} %pages.1), calls=%async_computation.1 | async-start | bytes 2097152 | tf_op jit(solution)/shard_map/all_to_all | solution.py:261
  38.9 13.8 %collective-permute-start.1 = (bf16[256,384]{1,0:T(8,128)(2,1)}, bf16[256,384]{1,0:T(8,128)(2,1)S(1)}, u32[]{:S(2)}, u32[]{:S(2)}) collective-permute-start(bf16[256,384]{1,0:T(8,128)(2,1)} %get-tuple-element.39), channel_id=1, source_target_pairs={{0,1},{1,2},{2,3},{3,0},{4,5},{5,6},{6,7},{7,4},{8,9},{9,10},{10,1... | collective-permute-start | bytes 589832 | tf_op jit(solution)/shard_map/ppermute | solution.py:228
  40.9 11.8 %collective-permute-start.2 = (bf16[256,384]{1,0:T(8,128)(2,1)}, bf16[256,384]{1,0:T(8,128)(2,1)S(1)}, u32[]{:S(2)}, u32[]{:S(2)}) collective-permute-start(bf16[256,384]{1,0:T(8,128)(2,1)} %get-tuple-element.40), channel_id=1, source_target_pairs={{0,2},{1,3},{2,0},{3,1},{4,6},{5,7},{6,4},{7,5},{8,10},{9,11},{10,... | collective-permute-start | bytes 589832 | tf_op jit(solution)/shard_map/ppermute | solution.py:228
  44.9 10.8 %collective-permute-start.3 = (bf16[256,384]{1,0:T(8,128)(2,1)S(1)}, bf16[256,384]{1,0:T(8,128)(2,1)S(1)}, u32[]{:S(2)}, u32[]{:S(2)}) collective-permute-start(bf16[256,384]{1,0:T(8,128)(2,1)S(1)} %copy-done.2), channel_id=1, source_target_pairs={{0,3},{1,0},{2,1},{3,2},{4,7},{5,4},{6,5},{7,6},{8,11},{9,8},{10,9... | collective-permute-start | bytes 589832 | tf_op jit(solution)/shard_map/ppermute | solution.py:228
  48.8 34.5 %collective-permute-start.8 = (bf16[1536,384]{1,0:T(8,128)(2,1)}, bf16[1536,384]{1,0:T(8,128)(2,1)S(1)}, u32[]{:S(2)}, u32[]{:S(2)}) collective-permute-start(bf16[1536,384]{1,0:T(8,128)(2,1)} %collective-permute-done.refs_5_), channel_id=1, source_target_pairs={{0,1},{1,2},{2,3},{3,0},{4,7},{5,4},{6,5},{7,6},{8,9},{9,10},{10,1... | collective-permute-start | bytes 3538952 | tf_op jit(solution)/shard_map/ppermute | solution.py:269
  50.7 32.5 %collective-permute-start.7 = (bf16[1536,384]{1,0:T(8,128)(2,1)}, bf16[1536,384]{1,0:T(8,128)(2,1)}, u32[]{:S(2)}, u32[]{:S(2)}) collective-permute-start(bf16[1536,384]{1,0:T(8,128)(2,1)} %collective-permute-done.refs_5_), channel_id=1, source_target_pairs={{0,4},{4,0},{8,12},{12,8},{16,20},{20,16},{24,28},{28,24},{32,36},... | collective-permute-start | bytes 3538952 | tf_op jit(solution)/shard_map/ppermute | solution.py:268
  66.2 10.3 %collective-permute-start.4 = (bf16[272,384]{1,0:T(8,128)(2,1)}, bf16[272,384]{1,0:T(8,128)(2,1)S(1)}, u32[]{:S(2)}, u32[]{:S(2)}) collective-permute-start(bf16[272,384]{1,0:T(8,128)(2,1)} %get-tuple-element.43), channel_id=1, source_target_pairs={{0,1},{1,2},{2,3},{3,0},{4,5},{5,6},{6,7},{7,4},{8,9},{9,10},{10,1... | collective-permute-start | bytes 626696 | tf_op jit(solution)/shard_map/ppermute | solution.py:228
  69.4 11.3 %collective-permute-start.5 = (bf16[272,384]{1,0:T(8,128)(2,1)}, bf16[272,384]{1,0:T(8,128)(2,1)S(1)}, u32[]{:S(2)}, u32[]{:S(2)}) collective-permute-start(bf16[272,384]{1,0:T(8,128)(2,1)} %get-tuple-element.44), channel_id=1, source_target_pairs={{0,2},{1,3},{2,0},{3,1},{4,6},{5,7},{6,4},{7,5},{8,10},{9,11},{10,... | collective-permute-start | bytes 626696 | tf_op jit(solution)/shard_map/ppermute | solution.py:228
  73.1 10.1 %collective-permute-start.6 = (bf16[272,384]{1,0:T(8,128)(2,1)}, bf16[272,384]{1,0:T(8,128)(2,1)S(1)}, u32[]{:S(2)}, u32[]{:S(2)}) collective-permute-start(bf16[272,384]{1,0:T(8,128)(2,1)} %get-tuple-element.45), channel_id=1, source_target_pairs={{0,3},{1,0},{2,1},{3,2},{4,7},{5,4},{6,5},{7,6},{8,11},{9,8},{10,9... | collective-permute-start | bytes 626696 | tf_op jit(solution)/shard_map/ppermute | solution.py:228
  83.2 1.0 %copy-start.1 = (bf16[1536,384]{1,0:T(8,128)(2,1)}, bf16[1536,384]{1,0:T(8,128)(2,1)S(1)}, u32[]{:S(2)}) copy-start(bf16[1536,384]{1,0:T(8,128)(2,1)S(1)} %collective-permute-done.8.refs_7_) | copy-start | bytes 3538948

commit v4 on v3

--- a/solution.py
+++ b/solution.py
@@ -39,22 +39,29 @@
 
 def page_kernel(slot_ref, kv_ref, out_ref):
     out_ref[...] = jnp.zeros(out_ref.shape, out_ref.dtype)
-    rows = lax.broadcasted_iota(jnp.int32, (2 * LANES, 2 * LANES), 0)
-    cols = lax.broadcasted_iota(jnp.int32, (2 * LANES, 2 * LANES), 1)
-    weave = (cols == (rows % 2) * LANES + rows // 2).astype(f32).astype(bf16)
+    chunk = LANES // 2
+    rows = lax.broadcasted_iota(jnp.int32, (2 * chunk, 2 * chunk), 0)
+    cols = lax.broadcasted_iota(jnp.int32, (2 * chunk, 2 * chunk), 1)
+    weave = (cols == (rows % 2) * chunk + rows // 2).astype(f32).astype(bf16)
     page_rows = 2 * PAGE_TOKENS
-    per_chunk = LANES // PAGE_TOKENS
-    chunks_per_block = kv_ref.shape[1] // LANES
-    for block in range(kv_ref.shape[0]):
-        for part in range(chunks_per_block):
-            here = pl.ds(part * LANES, LANES)
-            both = jnp.concatenate(
-                [kv_ref[block, here, :LANES], kv_ref[block, here, LANES:]], axis=0
-            )
-            woven = jnp.dot(weave, both, preferred_element_type=f32).astype(bf16)
-            for p in range(per_chunk):
-                page = (block * chunks_per_block + part) * per_chunk + p
-                out_ref[slot_ref[page]] = woven[p * page_rows : (p + 1) * page_rows]
+    per_chunk = chunk // PAGE_TOKENS
+    sides = [
+        jnp.concatenate(
+            [
+                kv_ref[block, part * chunk : (part + 1) * chunk, :LANES],
+                kv_ref[block, part * chunk : (part + 1) * chunk, LANES:],
+            ],
+            axis=0,
+        )
+        for block in range(kv_ref.shape[0])
+        for part in range(kv_ref.shape[1] // chunk)
+    ]
+    woven = jnp.dot(weave, jnp.concatenate(sides, axis=1), preferred_element_type=f32).astype(bf16)
+    for i in range(len(sides)):
+        for p in range(per_chunk):
+            out_ref[slot_ref[i * per_chunk + p]] = woven[
+                p * page_rows : (p + 1) * page_rows, i * LANES : (i + 1) * LANES
+            ]
 
 
 def variants(pair, lane):
@@ -250,7 +257,8 @@
         ((dest[:, None] == dest[None, :]) & (index[None, :] < index[:, None])).astype(jnp.int32), axis=1
     )
     lane_cap = max(2, 2 * pages // n_req)
-    slots, q_parts = lax.optimization_barrier((dest * lane_cap + lane, q_parts))
+    slots, q_parts = lax.optimization_barrier(((n_req - 1 - dest) * lane_cap + lane, q_parts))
+    order = [list(range(n_req - 1, -1, -1))]
     outgoing = pl.pallas_call(
         page_kernel,
         out_shape=jax.ShapeDtypeStruct((n_req * lane_cap, 2 * PAGE_TOKENS, kv_cols), bf16),
@@ -258,7 +266,8 @@
         out_specs=vmem,
         name="pages",
     )(slots, near(kv))
-    store = lax.all_to_all(outgoing, "req", 0, 0, tiled=True)
+    store = lax.all_to_all(outgoing, "req", 0, 0, axis_index_groups=order, tiled=True)
+    store = jnp.flip(store.reshape(n_req, lane_cap, PAGE_TOKENS, 2, kv_cols), 0)
     w_beside = lax.ppermute(w_source, ("req", "ctx"), ring)
     outgoing, w_beside = lax.optimization_barrier((outgoing, w_beside))
     w_beside, q_parts = lax.optimization_barrier((w_beside, q_parts))

time: 96.6 us -> 93.8 us (0.971)
  the two profiles are of different devices: /device:TPU:10 before, /device:TPU:40 now
where the time goes in v4:
time: 93.8 us; the launch traced here: 93.2 us
  starting transfers between devices  52.7 us (56%)
  Pallas kernels  22.5 us (24%)
  waiting for transfers between devices  13.8 us (15%)
  local copies, waits for them, and re-layouts  2.74 us (3%)
    ppermute x6, starting transfers between devices, shards(): lax.ppermute(a, 'ctx', [(i, (i + shift) % n_ctx) for i in range(n_ctx)])  20.3 us
    all_to_all x1, starting transfers between devices, shards(): lax.all_to_all(outgoing, 'req', 0, 0, axis_index_groups=order, tiled=True)  20.2 us
    pallas_call x1, Pallas kernels, shards(): pl.pallas_call(attention_kernel, out_shape=[jax.ShapeDtypeStruct((rows +...  10.5 us
    ppermute x6, waiting for transfers between devices, shards(): lax.ppermute(a, 'ctx', [(i, (i + shift) % n_ctx) for i in range(n_ctx)])  9.4 us
    pallas_call x1, Pallas kernels, shards(): pl.pallas_call(out_kernel, out_shape=(jax.ShapeDtypeStruct(prefill_residu...  5.8 us
    all_to_all x1, starting transfers between devices, shards(): kv = lax.all_to_all(kv_parts, 'ctx', 0, 0, tiled=True)  4.91 us
    ppermute x1, starting transfers between devices, shards(): w_beside = lax.ppermute(w_source, ('req', 'ctx'), ring)  3.36 us
    all_to_all x1, waiting for transfers between devices, shards(): kv = lax.all_to_all(kv_parts, 'ctx', 0, 0, tiled=True)  3.32 us
  transfers between devices with their start and end apart: 11, of which 5 were waited for; matrix products, arithmetic and copies ran while one was open for 1% of the time, Pallas kernels for 22%

profile of v4, /device:TPU:40, one launch (start us, length us, event | category | flops | bytes accessed | tf_op | source)
XLA Modules:
  0.0 93.2 jit_solution(12150221637412795777)
XLA Ops:
  0.7 2.0 %pair.1 = bf16[4,256,256]{2,1,0:T(8,128)(2,1)} custom-call(bf16[256,512]{1,0:T(8,128)(2,1)} %k_ref.1, bf16[256,512]{1,0:T(8,128)(2,1)} %v_ref.1), custom_call_target="tpu_custom_call" | custom-call | tf_op jit(solution)/shard_map/pair/pallas_call | solution.py:225
  2.7 4.9 %all-to-all-start = ((bf16[4,256,256]{2,1,0:T(8,128)(2,1)}), bf16[4,256,256]{2,1,0:T(8,128)(2,1)S(1)}, u32[]{:S(2)}, u32[]{:S(2)}) async-start(bf16[4,256,256]{2,1,0:T(8,128)(2,1)} %pair.1), calls=%async_computation | async-start | bytes 1048576 | tf_op jit(solution)/shard_map/all_to_all | solution.py:232
  7.6 3.4 %collective-permute-start = (bf16[1536,384]{1,0:T(8,128)(2,1)S(1)}, bf16[1536,384]{1,0:T(8,128)(2,1)}, u32[]{:S(2)}, u32[]{:S(2)}) collective-permute-start(bf16[1536,384]{1,0:T(8,128)(2,1)S(1)} %copy-done), channel_id=1, source_target_pairs={{0,1},{1,2},{2,3},{3,0},{4,7},{5,4},{6,5},{7,6},{8,9},{9,10},{10,1... | collective-permute-start | bytes 3538952 | tf_op jit(solution)/shard_map/ppermute | solution.py:271
  11.1 2.1 %split.1 = (bf16[256,384]{1,0:T(8,128)(2,1)}, bf16[256,384]{1,0:T(8,128)(2,1)}, bf16[256,384]{1,0:T(8,128)(2,1)}, bf16[256,384]{1,0:T(8,128)(2,1)}) custom-call(s32[1]{0:T(128)} %bitcast.place_ref, bf16[256,1536]{1,0:T(8,128)(2,1)} %q_ref), custom_call_target="tpu_custom_call" | custom-call | tf_op jit(solution)/shard_map/split/pallas_call | solution.py:237
  13.2 0.5 multiply_add_fusion.slot_ref
  13.7 3.3 %all-to-all-done.kv_ref.refs_4_ = bf16[4,256,256]{2,1,0:T(8,128)(2,1)S(1)} async-done(((bf16[4,256,256]{2,1,0:T(8,128)(2,1)}), bf16[4,256,256]{2,1,0:T(8,128)(2,1)S(1)}, u32[]{:S(2)}, u32[]{:S(2)}) %all-to-all-start) | async-done | bytes 524320 | tf_op jit(solution)/shard_map/all_to_all | solution.py:232
  17.1 2.1 %pages.1 = bf16[256,16,128]{2,1,0:T(8,128)(2,1)} custom-call(s32[128]{0:T(128)} %multiply_add_fusion.slot_ref, bf16[4,256,256]{2,1,0:T(8,128)(2,1)S(1)} %all-to-all-done.kv_ref.refs_4_), custom_call_target="tpu_custom_call" | custom-call | tf_op jit(solution)/shard_map/pages/pallas_call | solution.py:262
  19.1 20.2 %all-to-all-start.1 = ((bf16[256,16,128]{2,1,0:T(8,128)(2,1)}), bf16[256,16,128]{2,1,0:T(8,128)(2,1)S(1)}, u32[]{:S(2)}, u32[]{:S(2)}) async-start(bf16[256,16,128]{2,1,0:T(8,128)(2,1)} %pages.1), calls=%async_computation.1 | async-start | bytes 2097152 | tf_op jit(solution)/shard_map/all_to_all | solution.py:269
  39.3 1.9 %collective-permute-start.1 = (bf16[256,384]{1,0:T(8,128)(2,1)}, bf16[256,384]{1,0:T(8,128)(2,1)S(1)}, u32[]{:S(2)}, u32[]{:S(2)}) collective-permute-start(bf16[256,384]{1,0:T(8,128)(2,1)} %get-tuple-element.39), channel_id=1, source_target_pairs={{0,1},{1,2},{2,3},{3,0},{4,5},{5,6},{6,7},{7,4},{8,9},{9,10},{10,1... | collective-permute-start | bytes 589832 | tf_op jit(solution)/shard_map/ppermute | solution.py:235
  41.2 4.0 %collective-permute-start.2 = (bf16[256,384]{1,0:T(8,128)(2,1)}, bf16[256,384]{1,0:T(8,128)(2,1)S(1)}, u32[]{:S(2)}, u32[]{:S(2)}) collective-permute-start(bf16[256,384]{1,0:T(8,128)(2,1)} %get-tuple-element.40), channel_id=1, source_target_pairs={{0,2},{1,3},{2,0},{3,1},{4,6},{5,7},{6,4},{7,5},{8,10},{9,11},{10,... | collective-permute-start | bytes 589832 | tf_op jit(solution)/shard_map/ppermute | solution.py:235
  45.3 3.9 %collective-permute-start.3 = (bf16[256,384]{1,0:T(8,128)(2,1)S(1)}, bf16[256,384]{1,0:T(8,128)(2,1)S(1)}, u32[]{:S(2)}, u32[]{:S(2)}) collective-permute-start(bf16[256,384]{1,0:T(8,128)(2,1)S(1)} %copy-done.2), channel_id=1, source_target_pairs={{0,3},{1,0},{2,1},{3,2},{4,7},{5,4},{6,5},{7,6},{8,11},{9,8},{10,9... | collective-permute-start | bytes 589832 | tf_op jit(solution)/shard_map/ppermute | solution.py:235
  49.2 2.0 %collective-permute-start.8 = (bf16[1536,384]{1,0:T(8,128)(2,1)}, bf16[1536,384]{1,0:T(8,128)(2,1)S(1)}, u32[]{:S(2)}, u32[]{:S(2)}) collective-permute-start(bf16[1536,384]{1,0:T(8,128)(2,1)} %collective-permute-done.refs_5_), channel_id=1, source_target_pairs={{0,1},{1,2},{2,3},{3,0},{4,7},{5,4},{6,5},{7,6},{8,9},{9,10},{10,1... | collective-permute-start | bytes 3538952 | tf_op jit(solution)/shard_map/ppermute | solution.py:278
  51.1 1.9 %collective-permute-start.7 = (bf16[1536,384]{1,0:T(8,128)(2,1)}, bf16[1536,384]{1,0:T(8,128)(2,1)}, u32[]{:S(2)}, u32[]{:S(2)}) collective-permute-start(bf16[1536,384]{1,0:T(8,128)(2,1)} %collective-permute-done.refs_5_), channel_id=1, source_target_pairs={{0,4},{4,0},{8,12},{12,8},{16,20},{20,16},{24,28},{28,24},{32,36},... | collective-permute-start | bytes 3538952 | tf_op jit(solution)/shard_map/ppermute | solution.py:277
  53.1 3.0 %collective-permute-done.3.refs_3_ = bf16[256,384]{1,0:T(8,128)(2,1)S(1)} collective-permute-done((bf16[256,384]{1,0:T(8,128)(2,1)S(1)}, bf16[256,384]{1,0:T(8,128)(2,1)S(1)}, u32[]{:S(2)}, u32[]{:S(2)}) %collective-permute-start.3) | collective-permute-done | bytes 196640 | tf_op jit(solution)/shard_map/ppermute | solution.py:235
  56.0 10.5 %attend.1 = (bf16[272,384]{1,0:T(8,128)(2,1)}, bf16[272,384]{1,0:T(8,128)(2,1)}, bf16[272,384]{1,0:T(8,128)(2,1)}, bf16[272,384]{1,0:T(8,128)(2,1)}) custom-call(s32[1]{0:T(128)} %bitcast.place_ref, s32[1,3]{1,0:T(1,128)} %len_ref.1, bf16[256,384]{1,0:T(8,128)(2,1)} %get-tuple-element.38.refs_0_, bf16[256,384]{1,0:T(8,128)(2,1)S(1)} %collective-permute-done.1.refs_1_, ...), custom_call_target="tpu_custom_call" | custom-call | flops 30000001024 | tf_op jit(solution)/shard_map/attend/pallas_call | solution.py:280
  66.6 3.3 %collective-permute-start.4 = (bf16[272,384]{1,0:T(8,128)(2,1)}, bf16[272,384]{1,0:T(8,128)(2,1)S(1)}, u32[]{:S(2)}, u32[]{:S(2)}) collective-permute-start(bf16[272,384]{1,0:T(8,128)(2,1)} %get-tuple-element.43), channel_id=1, source_target_pairs={{0,1},{1,2},{2,3},{3,0},{4,5},{5,6},{6,7},{7,4},{8,9},{9,10},{10,1... | collective-permute-start | bytes 626696 | tf_op jit(solution)/shard_map/ppermute | solution.py:235
  69.8 3.6 %collective-permute-start.5 = (bf16[272,384]{1,0:T(8,128)(2,1)}, bf16[272,384]{1,0:T(8,128)(2,1)S(1)}, u32[]{:S(2)}, u32[]{:S(2)}) collective-permute-start(bf16[272,384]{1,0:T(8,128)(2,1)} %get-tuple-element.44), channel_id=1, source_target_pairs={{0,2},{1,3},{2,0},{3,1},{4,6},{5,7},{6,4},{7,5},{8,10},{9,11},{10,... | collective-permute-start | bytes 626696 | tf_op jit(solution)/shard_map/ppermute | solution.py:235
  73.4 3.7 %collective-permute-start.6 = (bf16[272,384]{1,0:T(8,128)(2,1)}, bf16[272,384]{1,0:T(8,128)(2,1)S(1)}, u32[]{:S(2)}, u32[]{:S(2)}) collective-permute-start(bf16[272,384]{1,0:T(8,128)(2,1)} %get-tuple-element.45), channel_id=1, source_target_pairs={{0,3},{1,0},{2,1},{3,2},{4,7},{5,4},{6,5},{7,6},{8,11},{9,8},{10,9... | collective-permute-start | bytes 626696 | tf_op jit(solution)/shard_map/ppermute | solution.py:235
  77.1 4.0 %collective-permute-done.5.refs_2_ = bf16[272,384]{1,0:T(8,128)(2,1)S(1)} collective-permute-done((bf16[272,384]{1,0:T(8,128)(2,1)}, bf16[272,384]{1,0:T(8,128)(2,1)S(1)}, u32[]{:S(2)}, u32[]{:S(2)}) %collective-permute-start.5) | collective-permute-done | bytes 208928 | tf_op jit(solution)/shard_map/ppermute | solution.py:235
  81.2 2.4 %collective-permute-done.6.refs_3_ = bf16[272,384]{1,0:T(8,128)(2,1)S(1)} collective-permute-done((bf16[272,384]{1,0:T(8,128)(2,1)}, bf16[272,384]{1,0:T(8,128)(2,1)S(1)}, u32[]{:S(2)}, u32[]{:S(2)}) %collective-permute-start.6) | collective-permute-done | bytes 208928 | tf_op jit(solution)/shard_map/ppermute | solution.py:235
  83.6 1.0 %copy-done.1 = bf16[1536,384]{1,0:T(8,128)(2,1)} copy-done((bf16[1536,384]{1,0:T(8,128)(2,1)}, bf16[1536,384]{1,0:T(8,128)(2,1)S(1)}, u32[]{:S(2)}) %copy-start.1) | copy-done | bytes 1179672
  84.6 5.8 %project.1 = (bf16[256,1536]{1,0:T(8,128)(2,1)}, bf16[1,3,384]{2,1,0:T(4,128)(2,1)}) custom-call(s32[1]{0:T(128)} %bitcast.place_ref, s32[1]{0:T(128)} %bitcast.1.core_ref, bf16[272,384]{1,0:T(8,128)(2,1)} %get-tuple-element.42.refs_0_, bf16[272,384]{1,0:T(8,128)(2,1)S(1)} %collective-permute-done.4.refs_1_, ...), custom_call_target="tpu_custom_call" | custom-call | tf_op jit(solution)/shard_map/project/pallas_call | solution.py:293
  90.4 1.1 %all-to-all-done.1 = bf16[256,16,128]{2,1,0:T(8,128)(2,1)S(1)} async-done(((bf16[256,16,128]{2,1,0:T(8,128)(2,1)}), bf16[256,16,128]{2,1,0:T(8,128)(2,1)S(1)}, u32[]{:S(2)}, u32[]{:S(2)}) %all-to-all-start.1) | async-done | bytes 1048608 | tf_op jit(solution)/shard_map/all_to_all | solution.py:269
  91.5 1.7 %rev.4 = bf16[128,2,8,2,128]{4,3,2,1,0:T(2,128)(2,1)} reverse(bf16[128,2,8,2,128]{4,3,2,1,0:T(2,128)(2,1)S(1)} %bitcast.6), dimensions={0} | reverse | bytes 2097152 | tf_op jit(solution)/shard_map/jit(_flip)/rev | solution.py:270
  (14 shorter events, 0.2 us)
Async XLA Ops:
  0.6 6.9 %copy-start = (bf16[1536,384]{1,0:T(8,128)(2,1)S(1)}, bf16[1536,384]{1,0:T(8,128)(2,1)}, u32[]{:S(2)}) copy-start(bf16[1536,384]{1,0:T(8,128)(2,1)} %refs_4_.1) | copy-start | bytes 3538948
  0.6 10.3 %copy-start.3 = (s32[1,128,1]{1,2,0:T(1,128)S(1)}, s32[1,128,1]{1,2,0:T(1,128)}, u32[]{:S(2)}) copy-start(s32[1,128,1]{1,2,0:T(1,128)} %param.17) | copy-start | bytes 1540
  2.7 14.4 %all-to-all-start = ((bf16[4,256,256]{2,1,0:T(8,128)(2,1)}), bf16[4,256,256]{2,1,0:T(8,128)(2,1)S(1)}, u32[]{:S(2)}, u32[]{:S(2)}) async-start(bf16[4,256,256]{2,1,0:T(8,128)(2,1)} %pair.1), calls=%async_computation | async-start | bytes 1048576 | tf_op jit(solution)/shard_map/all_to_all | solution.py:232
  7.6 31.7 %collective-permute-start = (bf16[1536,384]{1,0:T(8,128)(2,1)S(1)}, bf16[1536,384]{1,0:T(8,128)(2,1)}, u32[]{:S(2)}, u32[]{:S(2)}) collective-permute-start(bf16[1536,384]{1,0:T(8,128)(2,1)S(1)} %copy-done), channel_id=1, source_target_pairs={{0,1},{1,2},{2,3},{3,0},{4,7},{5,4},{6,5},{7,6},{8,9},{9,10},{10,1... | collective-permute-start | bytes 3538952 | tf_op jit(solution)/shard_map/ppermute | solution.py:271
  19.1 26.2 %copy-start.2 = (bf16[256,384]{1,0:T(8,128)(2,1)S(1)}, bf16[256,384]{1,0:T(8,128)(2,1)}, u32[]{:S(2)}) copy-start(bf16[256,384]{1,0:T(8,128)(2,1)} %get-tuple-element.41) | copy-start | bytes 589828
  19.1 72.4 %all-to-all-start.1 = ((bf16[256,16,128]{2,1,0:T(8,128)(2,1)}), bf16[256,16,128]{2,1,0:T(8,128)(2,1)S(1)}, u32[]{:S(2)}, u32[]{:S(2)}) async-start(bf16[256,16,128]{2,1,0:T(8,128)(2,1)} %pages.1), calls=%async_computation.1 | async-start | bytes 2097152 | tf_op jit(solution)/shard_map/all_to_all | solution.py:269
  39.3 13.8 %collective-permute-start.1 = (bf16[256,384]{1,0:T(8,128)(2,1)}, bf16[256,384]{1,0:T(8,128)(2,1)S(1)}, u32[]{:S(2)}, u32[]{:S(2)}) collective-permute-start(bf16[256,384]{1,0:T(8,128)(2,1)} %get-tuple-element.39), channel_id=1, source_target_pairs={{0,1},{1,2},{2,3},{3,0},{4,5},{5,6},{6,7},{7,4},{8,9},{9,10},{10,1... | collective-permute-start | bytes 589832 | tf_op jit(solution)/shard_map/ppermute | solution.py:235
  41.2 11.8 %collective-permute-start.2 = (bf16[256,384]{1,0:T(8,128)(2,1)}, bf16[256,384]{1,0:T(8,128)(2,1)S(1)}, u32[]{:S(2)}, u32[]{:S(2)}) collective-permute-start(bf16[256,384]{1,0:T(8,128)(2,1)} %get-tuple-element.40), channel_id=1, source_target_pairs={{0,2},{1,3},{2,0},{3,1},{4,6},{5,7},{6,4},{7,5},{8,10},{9,11},{10,... | collective-permute-start | bytes 589832 | tf_op jit(solution)/shard_map/ppermute | solution.py:235
  45.3 10.8 %collective-permute-start.3 = (bf16[256,384]{1,0:T(8,128)(2,1)S(1)}, bf16[256,384]{1,0:T(8,128)(2,1)S(1)}, u32[]{:S(2)}, u32[]{:S(2)}) collective-permute-start(bf16[256,384]{1,0:T(8,128)(2,1)S(1)} %copy-done.2), channel_id=1, source_target_pairs={{0,3},{1,0},{2,1},{3,2},{4,7},{5,4},{6,5},{7,6},{8,11},{9,8},{10,9... | collective-permute-start | bytes 589832 | tf_op jit(solution)/shard_map/ppermute | solution.py:235
  49.2 34.4 %collective-permute-start.8 = (bf16[1536,384]{1,0:T(8,128)(2,1)}, bf16[1536,384]{1,0:T(8,128)(2,1)S(1)}, u32[]{:S(2)}, u32[]{:S(2)}) collective-permute-start(bf16[1536,384]{1,0:T(8,128)(2,1)} %collective-permute-done.refs_5_), channel_id=1, source_target_pairs={{0,1},{1,2},{2,3},{3,0},{4,7},{5,4},{6,5},{7,6},{8,9},{9,10},{10,1... | collective-permute-start | bytes 3538952 | tf_op jit(solution)/shard_map/ppermute | solution.py:278
  51.1 32.4 %collective-permute-start.7 = (bf16[1536,384]{1,0:T(8,128)(2,1)}, bf16[1536,384]{1,0:T(8,128)(2,1)}, u32[]{:S(2)}, u32[]{:S(2)}) collective-permute-start(bf16[1536,384]{1,0:T(8,128)(2,1)} %collective-permute-done.refs_5_), channel_id=1, source_target_pairs={{0,4},{4,0},{8,12},{12,8},{16,20},{20,16},{24,28},{28,24},{32,36},... | collective-permute-start | bytes 3538952 | tf_op jit(solution)/shard_map/ppermute | solution.py:277
  66.6 10.6 %collective-permute-start.4 = (bf16[272,384]{1,0:T(8,128)(2,1)}, bf16[272,384]{1,0:T(8,128)(2,1)S(1)}, u32[]{:S(2)}, u32[]{:S(2)}) collective-permute-start(bf16[272,384]{1,0:T(8,128)(2,1)} %get-tuple-element.43), channel_id=1, source_target_pairs={{0,1},{1,2},{2,3},{3,0},{4,5},{5,6},{6,7},{7,4},{8,9},{9,10},{10,1... | collective-permute-start | bytes 626696 | tf_op jit(solution)/shard_map/ppermute | solution.py:235
  69.8 11.3 %collective-permute-start.5 = (bf16[272,384]{1,0:T(8,128)(2,1)}, bf16[272,384]{1,0:T(8,128)(2,1)S(1)}, u32[]{:S(2)}, u32[]{:S(2)}) collective-permute-start(bf16[272,384]{1,0:T(8,128)(2,1)} %get-tuple-element.44), channel_id=1, source_target_pairs={{0,2},{1,3},{2,0},{3,1},{4,6},{5,7},{6,4},{7,5},{8,10},{9,11},{10,... | collective-permute-start | bytes 626696 | tf_op jit(solution)/shard_map/ppermute | solution.py:235
  73.4 10.1 %collective-permute-start.6 = (bf16[272,384]{1,0:T(8,128)(2,1)}, bf16[272,384]{1,0:T(8,128)(2,1)S(1)}, u32[]{:S(2)}, u32[]{:S(2)}) collective-permute-start(bf16[272,384]{1,0:T(8,128)(2,1)} %get-tuple-element.45), channel_id=1, source_target_pairs={{0,3},{1,0},{2,1},{3,2},{4,7},{5,4},{6,5},{7,6},{8,11},{9,8},{10,9... | collective-permute-start | bytes 626696 | tf_op jit(solution)/shard_map/ppermute | solution.py:235
  83.6 1.0 %copy-start.1 = (bf16[1536,384]{1,0:T(8,128)(2,1)}, bf16[1536,384]{1,0:T(8,128)(2,1)S(1)}, u32[]{:S(2)}) copy-start(bf16[1536,384]{1,0:T(8,128)(2,1)S(1)} %collective-permute-done.8.refs_7_) | copy-start | bytes 3538948
